TPU v7x, 128 devices: a whole 4x4x4 slice. The times are simulated.
128 devices in a mesh: feat: 8 (over x, z_lo), seq: 16 (over z_hi, y, core).
Axes of the slice: x: 4, y: 4, z: 4 (z_hi: 2, z_lo: 2; z = z_hi * 2 + z_lo), core: 2. Of those that a mesh axis runs over, the one named last changes fastest.
Arguments:
- tokens: bfloat16 [8192, 8192], P('seq', 'feat'), may hold values from -6 to 6
- block_weights: bfloat16 [28672, 512], P('feat'), may hold values from -0.25 to 0.25
- left_factor: bfloat16 [28672, 256], P('feat'), may hold values from -0.09375 to 0.09375
- right_factor: bfloat16 [8192, 256], P('feat'), may hold values from -0.0625 to 0.0625
- pattern: int32 [224, 4], P('feat'), may hold values from 0 to 63, as said below
- cotangent: bfloat16 [8192, 28672], P('seq', 'feat'), may hold values from -6 to 6
Outputs:
- activated: bfloat16 [8192, 28672], P('seq', 'feat')
- grad_input: bfloat16 [16, 512, 8192], P('seq', 'feat')
- grad_blocks: float32 [28672, 512], P(('feat', 'seq'))
- grad_left: float32 [28672, 256], P(('feat', 'seq'))
- grad_right: float32 [8192, 256], P(('feat', 'seq'))
Inputs may be any that keep to these rules, and one draw needn't show every extreme that they name: For block row f, pattern[f, 0] // 8 equals (f * 8) // 224, and pattern[f, j] = pattern[f, 0] XOR ((64) >> j) for 1 <= j < 4.
All inputs are finite; a program needn't handle non-finite values.
Results may differ from a plain program's by a relative error of at most 0.0051.
Values may be sent and summed in bfloat16 or wider, within the bound.
A program may use at most 192 MiB of HBM per device.

v0:
```python
import math

import jax
import jax.numpy as jnp
from jax import lax
from jax.sharding import PartitionSpec as P

BLK = 128
LEVELS = 4


def from_partner(value, axis, distance):
    mask = 2**distance
    pairs = [(source, source ^ mask) for source in range(lax.axis_size(axis))]
    return lax.ppermute(value, axis, pairs)


def activation(values):
    return jax.nn.gelu(values, approximate=True)


def partner_bit(stride, local_blocks):
    return (stride // local_blocks).bit_length() - 1


def local(tokens, block_weights, left_factor, right_factor, pattern, cotangent):
    tok_rows, local_width = tokens.shape
    feat_count = lax.axis_size("feat")
    seq_count = lax.axis_size("seq")
    norm_scale = 1.0 / math.sqrt(tok_rows * seq_count)
    local_blocks = local_width // BLK
    all_blocks = local_blocks * feat_count
    row_blocks = pattern.shape[0]
    out_rows = block_weights.shape[0]
    weight_blocks = block_weights.reshape(row_blocks, BLK, LEVELS, BLK)
    strides = [0] + [all_blocks >> level for level in range(1, LEVELS)]
    pieces = []
    for level in range(LEVELS):
        bit_index = partner_bit(strides[level], local_blocks) if level > 0 else -1
        source = tokens if bit_index < 0 else from_partner(tokens, "feat", bit_index)
        local_ids = pattern[:, level] % local_blocks
        pieces.append(jnp.take(source.reshape(tok_rows, local_blocks, BLK), local_ids, axis=1))
    picked = jnp.stack(pieces, axis=2)
    sparse = jnp.einsum("tfli,foli->tfo", picked, weight_blocks, preferred_element_type=jnp.float32)
    latent_part = jnp.dot(tokens, right_factor, preferred_element_type=jnp.float32)
    latent = lax.psum(latent_part, "feat").astype(jnp.bfloat16)
    pre = sparse.reshape(tok_rows, out_rows) + jnp.einsum(
        "tr,or->to", latent, left_factor, preferred_element_type=jnp.float32
    )
    activated, slope = jax.vjp(activation, pre)
    grad_pre = slope(cotangent.astype(jnp.float32))[0].astype(jnp.bfloat16)
    back_part = jnp.einsum("to,or->tr", grad_pre, left_factor, preferred_element_type=jnp.float32)
    back_latent = lax.psum(back_part, "feat").astype(jnp.bfloat16)
    low_rank = jnp.einsum(
        "tr,ir->ti", back_latent, right_factor, preferred_element_type=jnp.float32
    )
    grad_rows = grad_pre.reshape(tok_rows, row_blocks, BLK)
    spread = jnp.einsum(
        "tfo,foli->tfli", grad_rows, weight_blocks, preferred_element_type=jnp.float32
    )
    summed_grad = low_rank
    for level in range(LEVELS):
        bit_index = partner_bit(strides[level], local_blocks) if level > 0 else -1
        local_ids = pattern[:, level] % local_blocks
        level_term = (
            jnp.zeros((tok_rows, local_blocks, BLK), jnp.float32)
            .at[:, local_ids, :]
            .add(spread[:, :, level, :])
        )
        level_term = level_term.reshape(tok_rows, local_width)
        if bit_index >= 0:
            level_term = from_partner(level_term, "feat", bit_index)
        summed_grad = summed_grad + level_term
    local_grad = summed_grad.astype(jnp.bfloat16)
    regrouped = lax.all_to_all(local_grad, "feat", split_axis=0, concat_axis=1, tiled=True)
    grad_input = regrouped.reshape(1, tok_rows // feat_count, feat_count * local_width)
    window = min(out_rows // seq_count * lax.axis_size("seq") // BLK + 2, row_blocks)
    product = jnp.einsum("tfo,tfli->foli", grad_rows, picked, preferred_element_type=jnp.float32)
    product = product.reshape(window * BLK, LEVELS * BLK) * norm_scale
    grad_blocks = lax.psum_scatter(product, "seq", scatter_dimension=0, tiled=True)
    left_term = (
        jnp.einsum("to,tr->or", grad_pre, latent, preferred_element_type=jnp.float32) * norm_scale
    )
    right_term = (
        jnp.einsum("ti,tr->ir", tokens, back_latent, preferred_element_type=jnp.float32)
        * norm_scale
    )
    grad_left, grad_right = (
        lax.psum_scatter(left_term, "seq", scatter_dimension=0, tiled=True),
        lax.psum_scatter(right_term, "seq", scatter_dimension=0, tiled=True),
    )
    return (activated.astype(jnp.bfloat16), grad_input, grad_blocks, grad_left, grad_right)


def solution(mesh):
    in_specs = (
        P("seq", "feat"),
        P("feat", None),
        P("feat", None),
        P("feat", None),
        P("feat", None),
        P("seq", "feat"),
    )
    out_specs = (
        P("seq", "feat"),
        P("seq", "feat", None),
        P(("feat", "seq"), None),
        P(("feat", "seq"), None),
        P(("feat", "seq"), None),
    )
    return jax.shard_map(local, mesh=mesh, in_specs=in_specs, out_specs=out_specs, check_vma=False)
```

profile of v0, /device:TPU:0, one launch (start us, length us, event | category | flops | bytes accessed | tf_op | source)
XLA Modules:
  0.0 451.6 jit_solution(5003942331406243700)
XLA Ops:
  19.3 6.3 %reshape.62 = bf16[28,128,4,128]{3,2,1,0:T(4,128)(2,1)} reshape(bf16[3584,512]{1,0:T(8,128)(2,1)} %param.9) | data formatting | bytes 7340032 | tf_op jit(solution)/shard_map/reshape | solution.py:35
  28.5 61.9 %all-reduce.2 = bf16[512,256]{1,0:T(8,128)(2,1)} all-reduce(f32[512,256]{1,0:T(8,128)S(1)} %fusion.36), channel_id=1, replica_groups=mesh['feat'=8,'seq'=16] {'feat'}, use_global_device_ids=true, to_apply=%region_0.2 | all-reduce | flops 131072 | bytes 786432 | tf_op jit(solution)/shard_map/psum | solution.py:46
  99.5 4.2 gather_fusion.3
  106.6 5.8 %select_bitcast_fusion = (bf16[512,28,1,128]{3,0,2,1:T(8,128)(2,1)S(1)}, bf16[512,28,1,128]{3,0,2,1:T(8,128)(2,1)}) fusion(bf16[28,512,128]{2,1,0:T(8,128)(2,1)} %gather_fusion.3, pred[28]{0:T(512)(128)(4,1)S(1)} %get-tuple-element.46, bf16[28,512,128]{2,1,0:T(8,128)(2,1)} %gather_fusion.2, pred[28]{0:T(512)(128)(4,1)S(1)} %get-tuple-element.48), kind=kLoop, calls=%fused_computation.32 | loop fusion | flops 3670016 | bytes 14680120 | tf_op jit(solution)/shard_map/stack | solution.py:43
  112.6 4.1 select_bitcast_fusion.2
  117.3 9.7 %fusion.11 = f32[28,512,128,1]{1,2,3,0:T(8,128)} fusion(bf16[28,128,4,128]{3,2,1,0:T(4,128)(2,1)S(1)} %copy-done.5, bf16[512,28,1,128]{3,0,2,1:T(8,128)(2,1)S(1)} %get-tuple-element.50, bf16[512,28,1,128]{3,0,2,1:T(8,128)(2,1)} %get-tuple-element.51, bf16[512,28,1,128]{3,0,2,1:T(8,128)(2,1)} %get-tuple-element.52, ...), kind=kOutput, calls=%fused_computation.38 | convolution fusion | flops 1901068288 | bytes 25690112 | tf_op jit(solution)/shard_map/tfli,foli->tfo/dot_general | solution.py:44
  127.0 8.5 %copy.63 = f32[512,3584]{1,0:T(8,128)} copy(f32[512,3584]{0,1:T(8,128)} %bitcast.128) | data formatting | bytes 14680064 | tf_op jit(solution)/shard_map/reshape | solution.py:47
  135.5 10.3 %fusion.2 = (bf16[512,3584]{1,0:T(8,128)(2,1)S(1)}, bf16[512,3584]{1,0:T(8,128)(2,1)}) fusion(bf16[512,3584]{1,0:T(8,128)(2,1)} %param.13, f32[512,3584]{1,0:T(8,128)} %copy.63, bf16[512,256]{1,0:T(8,128)(2,1)S(1)} %copy-done.10, bf16[3584,256]{1,0:T(8,128)(2,1)S(1)} %copy-done), kind=kOutput, calls=%fused_computation.16 | convolution fusion | flops 983564288 | bytes 20447232 | tf_op jit(solution)/shard_map/tr,or->to/dot_general | solution.py:47
  149.6 40.0 %all-reduce.3 = bf16[512,256]{1,0:T(8,128)(2,1)S(1)} all-reduce(f32[512,256]{1,0:T(8,128)} %fusion.37), channel_id=1, replica_groups=mesh['feat'=8,'seq'=16] {'feat'}, use_global_device_ids=true, to_apply=%region_1.3 | all-reduce | flops 131072 | bytes 786432 | tf_op jit(solution)/shard_map/psum | solution.py:53
  191.4 5.0 %convolution_multiply_fusion = f32[3584,256]{1,0:T(8,128)} fusion(bf16[512,3584]{1,0:T(8,128)(2,1)} %copy-done.7, bf16[512,256]{1,0:T(8,128)(2,1)S(1)} %copy-done.10), kind=kOutput, calls=%fused_computation.31 | convolution fusion | flops 940441600 | bytes 7602176 | tf_op jit(solution)/shard_map/to,tr->or/dot_general | solution.py:82
  196.5 6.0 %copy.64 = bf16[512,3584]{0,1:T(8,128)(2,1)} copy(bf16[512,3584]{1,0:T(8,128)(2,1)} %copy-done.7) | data formatting | bytes 7340032 | tf_op jit(solution)/shard_map/convert_element_type | solution.py:51
  202.5 10.9 %broadcast_multiply_fusion = f32[28,128,4,128]{3,1,2,0:T(8,128)} fusion(bf16[512,28,128,1]{0,2,3,1:T(8,128)(2,1)} %bitcast.126, bf16[512,28,1,128]{3,0,2,1:T(8,128)(2,1)} %copy-done.8, bf16[512,28,1,128]{3,0,2,1:T(8,128)(2,1)} %get-tuple-element.51, bf16[512,28,1,128]{3,0,2,1:T(8,128)(2,1)} %get-tuple-element.52, ...), kind=kOutput, calls=%fused_computation.36 | convolution fusion | flops 1939603456 | bytes 25690112 | tf_op jit(solution)/shard_map/tfo,tfli->foli/dot_general | solution.py:78
  213.4 9.2 %copy.72 = f32[28,128,4,128]{3,2,1,0:T(4,128)S(1)} copy(f32[28,128,4,128]{3,1,2,0:T(8,128)} %broadcast_multiply_fusion) | data formatting | bytes 14680064 | tf_op jit(solution)/shard_map/mul | solution.py:79
  226.4 17.0 %convolution_bitcast_fusion = f32[512,28,4,128]{3,0,2,1:T(8,128)} fusion(bf16[512,28,128,1]{0,2,3,1:T(8,128)(2,1)} %bitcast.127, bf16[28,128,4,128]{3,2,1,0:T(4,128)(2,1)} %reshape.62), kind=kOutput, calls=%fused_computation.9 | convolution fusion | flops 1879048192 | bytes 36700160 | tf_op jit(solution)/shard_map/tfo,foli->tfli/dot_general | solution.py:58
  243.4 20.2 %slice_bitcast_fusion.3 = (f32[28,512,128]{2,1,0:T(8,128)}, f32[28,512,128]{2,1,0:T(8,128)}, f32[28,512,128]{2,1,0:T(8,128)}, f32[28,512,128]{2,1,0:T(8,128)}) fusion(f32[512,28,4,128]{3,0,2,1:T(8,128)} %convolution_bitcast_fusion), kind=kLoop, calls=%fused_computation.28 | loop fusion | bytes 58720256 | tf_op jit(solution)/shard_map/squeeze | solution.py:68
  265.1 17.7 %scatter_fusion.1 = f32[512,8,128]{2,0,1:T(8,128)} fusion(f32[512,8,128]{2,0,1:T(8,128)} %broadcast.93.clone.2, s32[28]{0:T(128)S(1)} %get-tuple-element.41, f32[28,512,128]{2,1,0:T(8,128)} %get-tuple-element.37), kind=kCustom, calls=%fused_computation.5 | custom fusion | flops 1835008 | bytes 22020208 | tf_op jit(solution)/shard_map/scatter-add | solution.py:68
  287.6 17.3 %scatter_fusion.2 = f32[512,8,128]{2,0,1:T(8,128)} fusion(f32[512,8,128]{2,0,1:T(8,128)} %broadcast.93.clone.1, s32[28]{0:T(128)S(1)} %get-tuple-element.42, f32[28,512,128]{2,1,0:T(8,128)} %get-tuple-element.36), kind=kCustom, calls=%fused_computation.6 | custom fusion | flops 1835008 | bytes 22020208 | tf_op jit(solution)/shard_map/scatter-add | solution.py:68
  311.0 17.5 %scatter_fusion.3 = f32[512,8,128]{2,0,1:T(8,128)} fusion(f32[512,8,128]{2,0,1:T(8,128)} %broadcast.93.clone, s32[28]{0:T(128)S(1)} %get-tuple-element.43, f32[28,512,128]{2,1,0:T(8,128)} %get-tuple-element.35), kind=kCustom, calls=%fused_computation.7 | custom fusion | flops 1835008 | bytes 22020208 | tf_op jit(solution)/shard_map/scatter-add | solution.py:68
  335.9 17.3 %scatter_fusion = f32[512,8,128]{2,0,1:T(8,128)} fusion(f32[512,8,128]{2,0,1:T(8,128)} %broadcast.93.clone.3, s32[28]{0:T(128)S(1)} %get-tuple-element.40, f32[28,512,128]{2,1,0:T(8,128)} %get-tuple-element.34), kind=kCustom, calls=%fused_computation.4 | custom fusion | flops 1835008 | bytes 22020208 | tf_op jit(solution)/shard_map/scatter-add | solution.py:68
  353.1 12.1 %collective-permute-done.4 = f32[512,1024]{1,0:T(8,128)} collective-permute-done((f32[512,1024]{1,0:T(8,128)}, f32[512,1024]{1,0:T(8,128)}, u32[]{:S(2)}, u32[]{:S(2)}) %collective-permute-start.4) | collective-permute-done | bytes 2097184 | tf_op jit(solution)/shard_map/ppermute | solution.py:15
  365.2 9.5 %collective-permute-done.5 = f32[512,1024]{1,0:T(8,128)} collective-permute-done((f32[512,1024]{1,0:T(8,128)}, f32[512,1024]{1,0:T(8,128)}, u32[]{:S(2)}, u32[]{:S(2)}) %collective-permute-start.5) | collective-permute-done | bytes 2097184 | tf_op jit(solution)/shard_map/ppermute | solution.py:15
  374.8 4.2 fusion.16
  378.9 15.7 %all_to_all.16 = bf16[8,64,1024]{2,1,0:T(8,128)(2,1)S(1)} all-to-all(bf16[8,64,1024]{2,1,0:T(8,128)(2,1)S(1)} %bitcast.129), channel_id=1, replica_groups=mesh['feat'=8,'seq'=16] {'feat'}, dimensions={0} | all-to-all | bytes 2097152 | tf_op jit(solution)/shard_map/all_to_all | solution.py:75
  396.5 48.5 %reduce-scatter.6.cloned.1.call-done = f32[224,512]{1,0:T(8,128)} async-done(((f32[3584,512]{1,0:T(8,128)}), f32[224,512]{1,0:T(8,128)}) %reduce-scatter.6.cloned.1.call-update) | async-done | bytes 458768 | tf_op jit(solution)/shard_map/reduce_scatter | solution.py:80
  (70 shorter events, 58.7 us)
Async XLA Ops:
  7.2 128.3 %copy-start = (bf16[3584,256]{1,0:T(8,128)(2,1)S(1)}, bf16[3584,256]{1,0:T(8,128)(2,1)}, u32[]{:S(2)}) copy-start(bf16[3584,256]{1,0:T(8,128)(2,1)} %param.10) | copy-start | bytes 5505028
  7.2 10.5 %copy-start.11 = (s32[28,4]{0,1:T(4,128)S(1)}, s32[28,4]{0,1:T(4,128)}, u32[]{:S(2)}) copy-start(s32[28,4]{0,1:T(4,128)} %param.12) | copy-start | bytes 1348
  7.2 389.3 %reduce-scatter.10.cloned.1.call-start = ((), (), s32[]{:S(2)}) async-start(), calls=%async_computation.6 | async-start | bytes 1114112
  9.6 80.8 %collective-permute-start.1 = (bf16[512,1024]{0,1:T(8,128)(2,1)}, bf16[512,1024]{0,1:T(8,128)(2,1)}, u32[]{:S(2)}, u32[]{:S(2)}) collective-permute-start(bf16[512,1024]{0,1:T(8,128)(2,1)} %copy.54), channel_id=1, source_target_pairs={{0,32},{16,48},{32,0},{48,16},{64,96},{80,112},{96,64},{112,80},{1... | collective-permute-start | bytes 3145736 | tf_op jit(solution)/shard_map/ppermute | solution.py:15
  11.2 80.9 %collective-permute-start.2 = (bf16[512,1024]{0,1:T(8,128)(2,1)}, bf16[512,1024]{0,1:T(8,128)(2,1)}, u32[]{:S(2)}, u32[]{:S(2)}) collective-permute-start(bf16[512,1024]{0,1:T(8,128)(2,1)} %copy.54), channel_id=1, source_target_pairs={{0,16},{16,0},{32,48},{48,32},{64,80},{80,64},{96,112},{112,96},{1... | collective-permute-start | bytes 3145736 | tf_op jit(solution)/shard_map/ppermute | solution.py:15
  13.1 81.2 %collective-permute-start = (bf16[512,1024]{0,1:T(8,128)(2,1)}, bf16[512,1024]{0,1:T(8,128)(2,1)}, u32[]{:S(2)}, u32[]{:S(2)}) collective-permute-start(bf16[512,1024]{0,1:T(8,128)(2,1)} %copy.54), channel_id=1, source_target_pairs={{0,64},{16,80},{32,96},{48,112},{64,0},{80,16},{96,32},{112,48},{1... | collective-permute-start | bytes 3145736 | tf_op jit(solution)/shard_map/ppermute | solution.py:15
  99.5 4.2 copy-start.2
  106.6 5.8 %copy-start.3 = (bf16[28,512,128]{2,1,0:T(8,128)(2,1)S(1)}, bf16[28,512,128]{2,1,0:T(8,128)(2,1)}, u32[]{:S(2)}) copy-start(bf16[28,512,128]{2,1,0:T(8,128)(2,1)} %gather_fusion) | copy-start | bytes 11010052
  106.6 6.0 %copy-start.4 = (bf16[28,512,128]{2,1,0:T(8,128)(2,1)S(1)}, bf16[28,512,128]{2,1,0:T(8,128)(2,1)}, u32[]{:S(2)}) copy-start(bf16[28,512,128]{2,1,0:T(8,128)(2,1)} %gather_fusion.1) | copy-start | bytes 11010052
  112.4 4.9 %copy-start.8 = (bf16[512,28,1,128]{3,0,2,1:T(8,128)(2,1)}, bf16[512,28,1,128]{3,0,2,1:T(8,128)(2,1)S(1)}, u32[]{:S(2)}) copy-start(bf16[512,28,1,128]{3,0,2,1:T(8,128)(2,1)S(1)} %get-tuple-element.50) | copy-start | bytes 11010052
  112.6 4.7 %copy-start.5 = (bf16[28,128,4,128]{3,2,1,0:T(4,128)(2,1)S(1)}, bf16[28,128,4,128]{3,2,1,0:T(4,128)(2,1)}, u32[]{:S(2)}) copy-start(bf16[28,128,4,128]{3,2,1,0:T(4,128)(2,1)} %reshape.62) | copy-start | bytes 11010052
  127.0 8.5 %copy-start.10 = (bf16[512,256]{1,0:T(8,128)(2,1)S(1)}, bf16[512,256]{1,0:T(8,128)(2,1)}, u32[]{:S(2)}) copy-start(bf16[512,256]{1,0:T(8,128)(2,1)} %all-reduce.2) | copy-start | bytes 786436
  145.8 1.8 copy-start.7
  147.7 41.9 %copy-start.6 = (bf16[512,1024]{1,0:T(8,128)(2,1)S(1)}, bf16[512,1024]{1,0:T(8,128)(2,1)}, u32[]{:S(2)}) copy-start(bf16[512,1024]{1,0:T(8,128)(2,1)} %param.8) | copy-start | bytes 3145732
  191.3 205.2 %reduce-scatter.8.cloned.1.call-start = ((), (), s32[]{:S(2)}) async-start(), calls=%async_computation.5 | async-start | bytes 3899392 | tf_op jit(solution)/shard_map/reduce_scatter | solution.py:89
  196.4 248.6 %reduce-scatter.6.cloned.1.call-start = ((), (), s32[]{:S(2)}) async-start(), calls=%async_computation.4 | async-start | bytes 7798784 | tf_op jit(solution)/shard_map/reduce_scatter | solution.py:80
  286.1 67.0 %collective-permute-start.3 = (f32[512,1024]{1,0:T(8,128)}, f32[512,1024]{1,0:T(8,128)}, u32[]{:S(2)}, u32[]{:S(2)}) collective-permute-start(f32[512,1024]{1,0:T(8,128)} %copy_bitcast_fusion.3), channel_id=1, source_target_pairs={{0,64},{16,80},{32,96},{48,112},{64,0},{80,16},{96,32},{112,48},{1... | collective-permute-start | bytes 6291464 | tf_op jit(solution)/shard_map/ppermute | solution.py:15
  308.1 57.1 %collective-permute-start.4 = (f32[512,1024]{1,0:T(8,128)}, f32[512,1024]{1,0:T(8,128)}, u32[]{:S(2)}, u32[]{:S(2)}) collective-permute-start(f32[512,1024]{1,0:T(8,128)} %copy_bitcast_fusion.2), channel_id=1, source_target_pairs={{0,32},{16,48},{32,0},{48,16},{64,96},{80,112},{96,64},{112,80},{1... | collective-permute-start | bytes 6291464 | tf_op jit(solution)/shard_map/ppermute | solution.py:15
  331.7 43.0 %collective-permute-start.5 = (f32[512,1024]{1,0:T(8,128)}, f32[512,1024]{1,0:T(8,128)}, u32[]{:S(2)}, u32[]{:S(2)}) collective-permute-start(f32[512,1024]{1,0:T(8,128)} %copy_bitcast_fusion.1), channel_id=1, source_target_pairs={{0,16},{16,0},{32,48},{48,32},{64,80},{80,64},{96,112},{112,96},{1... | collective-permute-start | bytes 6291464 | tf_op jit(solution)/shard_map/ppermute | solution.py:15
  335.9 38.9 %copy-start.9 = (bf16[1024,256]{1,0:T(8,128)(2,1)S(1)}, bf16[1024,256]{1,0:T(8,128)(2,1)}, u32[]{:S(2)}) copy-start(bf16[1024,256]{1,0:T(8,128)(2,1)} %param.11) | copy-start | bytes 1572868
  374.8 70.3 %copy-start.1 = (bf16[3584,256]{1,0:T(8,128)(2,1)S(1)}, bf16[3584,256]{1,0:T(8,128)(2,1)}, u32[]{:S(2)}) copy-start(bf16[3584,256]{1,0:T(8,128)(2,1)} %param.10) | copy-start | bytes 5505028
Sparse Core Ops, SparseCore 0:
  191.4 66.7 reduce-scatter.9
  263.4 77.6 reduce-scatter.7
  346.5 98.5 reduce-scatter.5
where the time goes:
time: 453 us; the launch traced here: 452 us
  blocking collectives  118 us (26%)
  local copies, waits for them, and re-layouts  98.5 us (22%)
  other arithmetic  79.8 us (18%)
  waiting for transfers between devices  70.2 us (15%)
  matrix products  61.3 us (14%)
  between operations  13.9 us (3%)
  starting transfers between devices  10.4 us (2%)
    scatter-add x4, other arithmetic, local(): level_term = jnp.zeros((tok_rows, local_blocks, BLK), jnp.float32).at[:,...  69.8 us
    psum x1, blocking collectives, local(): latent = lax.psum(latent_part, 'feat').astype(jnp.bfloat16)  61.9 us
    reduce_scatter x1, waiting for transfers between devices, local(): lax.psum_scatter(product, 'seq', scatter_dimension=0, tiled=True)  48.5 us
    psum x1, blocking collectives, local(): back_latent = lax.psum(back_part, 'feat').astype(jnp.bfloat16)  40 us
    ppermute x6, waiting for transfers between devices, from_partner(): return lax.ppermute(value, axis, pairs)  21.6 us
    squeeze x1, local copies, waits for them, and re-layouts, local(): spread[:, :, level, :]  20.2 us
    dot_general x1, matrix products, local(): jnp.einsum('tfo,foli->tfli', grad_rows, weight_blocks, preferred_element_...  17 us
    all_to_all x1, blocking collectives, local(): lax.all_to_all(local_grad, 'feat', split_axis=0, concat_axis=1, tiled=True)  15.7 us
  transfers between devices with their start and end apart: 9, of which 3 were waited for; matrix products, arithmetic and copies ran while one was open for 40% of the time, Pallas kernels for 0%

commit v1 on v0

v1 whole, which is shorter than its diff:
```python
import functools
import math

import jax
import jax.numpy as jnp
from jax import lax
from jax.experimental import pallas as pl
from jax.experimental.pallas import tpu as pltpu
from jax.sharding import PartitionSpec as P

BLK = 128
LEVELS = 4
MESH = pl.DeviceIdType.MESH
F32 = jnp.float32
BF16 = jnp.bfloat16
VMEM_LIMIT = 60 * 1024 * 1024
CHUNKS = 8


def remote(src, dst, send_sem, recv_sem, feat, seq):
    return pltpu.make_async_remote_copy(
        src_ref=src,
        dst_ref=dst,
        send_sem=send_sem,
        recv_sem=recv_sem,
        device_id=(feat, seq),
        device_id_type=MESH,
    )


def feat_neighbours(p):
    x, z = p // 2, p % 2
    flipped = x + 1 - 2 * (x % 2)
    return 2 * flipped + z, 2 * (3 - x) + z, 2 * x + 1 - z


def greet(devices):
    barrier = pltpu.get_barrier_semaphore()
    for feat, seq in devices:
        pl.semaphore_signal(barrier, inc=1, device_id=(feat, seq), device_id_type=MESH)
    pl.semaphore_wait(barrier, len(devices))


def sum_over_feat(p, s, part, landed, shared, rs_send, rs_recv, ag_send, ag_recv):
    count = part.shape[0]
    rs = [
        remote(part.at[(p + k) % count], landed.at[k - 1], rs_send.at[k - 1], rs_recv.at[k - 1], (p + k) % count, s)
        for k in range(1, count)
    ]
    ag = [
        remote(shared.at[p], shared.at[p], ag_send.at[k - 1], ag_recv.at[k - 1], (p + k) % count, s)
        for k in range(1, count)
    ]

    def send():
        for copy in rs:
            copy.start()

    def share():
        total = part[p]
        for k, copy in enumerate(rs):
            copy.wait_recv()
            total = total + landed[k]
        shared[p] = total.astype(shared.dtype)
        for copy in ag:
            copy.start()

    def finish():
        for copy in ag:
            copy.wait_recv()

    def drain():
        for copy in rs + ag:
            copy.wait_send()

    return send, share, finish, drain


def exchange_kernel(
    tok, right, x1, x2, x3, lat, tokv, part, landed, shared,
    load_sem, x_send, x_recv, f_send, f_recv, z_send, z_recv, rs_send, rs_recv, ag_send, ag_recv,
):
    p, s = lax.axis_index("feat"), lax.axis_index("seq")
    side, back, up = feat_neighbours(p)
    feats, slab = part.shape[0], part.shape[1]
    rows = tok.shape[0] // CHUNKS
    load = pltpu.make_async_copy(tok, tokv, load_sem)
    load.start()
    greet([((p + k) % feats, s) for k in range(1, feats)])

    def at(ref, c):
        return ref.at[pl.ds(c * rows, rows), :]

    own = [remote(at(tok, c), at(x2, c), x_send.at[c], x_recv.at[c], side, s) for c in range(CHUNKS)]
    passed = [remote(at(x2, c), at(x1, c), f_send.at[c], f_recv.at[c], back, s) for c in range(CHUNKS)]
    across = [remote(at(tok, c), at(x3, c), z_send.at[c], z_recv.at[c], up, s) for c in range(CHUNKS)]
    send, share, finish, drain = sum_over_feat(p, s, part, landed, shared, rs_send, rs_recv, ag_send, ag_recv)
    own[0].start()
    across[0].start()
    load.wait()
    for q in range(feats):
        part[q] = jnp.dot(tokv[q * slab : (q + 1) * slab, :], right[...], preferred_element_type=F32)
    send()
    for c in range(1, CHUNKS):
        own[c].start()
        across[c].start()
    for c in range(CHUNKS):
        own[c].wait_recv()
        passed[c].start()
        if c == 3:
            share()
    finish()
    for q in range(feats):
        lat[q * slab : (q + 1) * slab, :] = shared[q]
    for c in range(CHUNKS):
        across[c].wait()
        own[c].wait_send()
        passed[c].wait()
    drain()


def exchange(tokens, right):
    rows, width = tokens.shape
    rank = right.shape[1]
    feats = lax.axis_size("feat")
    slab = rows // feats
    whole = jax.ShapeDtypeStruct((rows, width), BF16)
    any_spec = pl.BlockSpec(memory_space=pl.ANY)
    vmem_spec = pl.BlockSpec(memory_space=pltpu.VMEM)
    dma = pltpu.SemaphoreType.DMA
    return pl.pallas_call(
        exchange_kernel,
        out_shape=(whole, whole, whole, jax.ShapeDtypeStruct((rows, rank), BF16)),
        in_specs=[any_spec, vmem_spec],
        out_specs=(any_spec, any_spec, any_spec, vmem_spec),
        scratch_shapes=[
            pltpu.VMEM((rows, width), BF16),
            pltpu.VMEM((feats, slab, rank), F32),
            pltpu.VMEM((feats - 1, slab, rank), F32),
            pltpu.VMEM((feats, slab, rank), BF16),
            dma,
            dma((CHUNKS,)), dma((CHUNKS,)), dma((CHUNKS,)), dma((CHUNKS,)), dma((CHUNKS,)), dma((CHUNKS,)),
            dma((feats - 1,)), dma((feats - 1,)), dma((feats - 1,)), dma((feats - 1,)),
        ],
        compiler_params=pltpu.CompilerParams(collective_id=0, has_side_effects=True, vmem_limit_bytes=VMEM_LIMIT),
    )(tokens, right)


def rows_kernel(norm_scale, lid_ref, tok, x1, x2, x3, lat, w, left, cot, act, terms, back, grads, acc):
    f = pl.program_id(0)

    @pl.when(f == 0)
    def _():
        acc[...] = jnp.zeros_like(acc)
        back[...] = jnp.zeros_like(back)

    lid = lid_ref[f]
    col = pl.ds(pl.multiple_of(lid * BLK, BLK), BLK)
    xl = jnp.concatenate([tok[:, col], x1[:, col], x2[:, col], x3[:, col], lat[...]], axis=1)
    wl = jnp.concatenate([w[...], left[...]], axis=1)
    pre = lax.dot_general(xl, wl, (((1,), (1,)), ((), ())), preferred_element_type=F32)
    c = math.sqrt(2.0 / math.pi)
    square = pre * pre
    th = jnp.tanh(c * (pre + 0.044715 * (square * pre)))
    half = 0.5 + 0.5 * th
    act[...] = (pre * half).astype(BF16)
    slope = half + (0.5 * c) * pre * (1.0 - th * th) * (1.0 + (3.0 * 0.044715) * square)
    gp = (cot[...].astype(F32) * slope).astype(BF16)
    spread = jnp.dot(gp, wl, preferred_element_type=F32)
    wide = LEVELS * BLK
    acc[lid] += spread[:, :wide]
    back[...] += spread[:, wide:]
    grads[...] = (
        lax.dot_general(gp, xl, (((0,), (0,)), ((), ())), preferred_element_type=F32) * norm_scale
    ).astype(BF16)

    @pl.when(f == pl.num_programs(0) - 1)
    def _():
        for j in range(LEVELS):
            for b in range(acc.shape[0]):
                terms[j, :, b * BLK : (b + 1) * BLK] = acc[b, :, j * BLK : (j + 1) * BLK].astype(BF16)


def block_rows(lids, tokens, x1, x2, x3, latent, weights, left, cotangent, norm_scale):
    rows, width = tokens.shape
    out_rows, wide = weights.shape
    rank = left.shape[1]
    whole = pl.BlockSpec((rows, width), lambda f, lid: (0, 0))
    return pl.pallas_call(
        functools.partial(rows_kernel, norm_scale),
        grid_spec=pltpu.PrefetchScalarGridSpec(
            num_scalar_prefetch=1,
            grid=(out_rows // BLK,),
            in_specs=[
                whole, whole, whole, whole,
                pl.BlockSpec((rows, rank), lambda f, lid: (0, 0)),
                pl.BlockSpec((BLK, wide), lambda f, lid: (f, 0)),
                pl.BlockSpec((BLK, rank), lambda f, lid: (f, 0)),
                pl.BlockSpec((rows, BLK), lambda f, lid: (0, f)),
            ],
            out_specs=[
                pl.BlockSpec((rows, BLK), lambda f, lid: (0, f)),
                pl.BlockSpec((LEVELS, rows, width), lambda f, lid: (0, 0, 0)),
                pl.BlockSpec((rows, rank), lambda f, lid: (0, 0)),
                pl.BlockSpec((BLK, wide + rank), lambda f, lid: (f, 0)),
            ],
            scratch_shapes=[pltpu.VMEM((width // BLK, rows, wide), F32)],
        ),
        out_shape=(
            jax.ShapeDtypeStruct((rows, out_rows), BF16),
            jax.ShapeDtypeStruct((LEVELS, rows, width), BF16),
            jax.ShapeDtypeStruct((rows, rank), F32),
            jax.ShapeDtypeStruct((out_rows, wide + rank), BF16),
        ),
        compiler_params=pltpu.CompilerParams(vmem_limit_bytes=VMEM_LIMIT),
    )(lids, tokens, x1, x2, x3, latent, weights, left, cotangent)


def gather_kernel(
    norm_scale, terms, part, right, tok, grads, gin, gblocks, gleft, gright,
    landed, shared, backv, low, rx1, mid, rx2, rz, fin, a2a,
    crecv, q, ry2, ry1, zsend, zrecv, grsend, grrecv,
    rs_send, rs_recv, ag_send, ag_recv, x1s, x1r, x2s, x2r, zs, zr, as_, ar,
    cs, cr, y2s, y2r, y1s, y1r, hs, hr, gs, gr,
):
    p, s = lax.axis_index("feat"), lax.axis_index("seq")
    side, back, up = feat_neighbours(p)
    feats, slab = part.shape[0], part.shape[1]
    seqs = 16
    core, y, half = s % 2, (s // 2) % 4, s // 8
    piece = gblocks.shape[0]
    wide = gblocks.shape[1]

    def seq_at(half_, y_, core_):
        return half_ * 8 + y_ * 2 + core_

    greet(
        [((p + k) % feats, s) for k in range(1, feats)] + [(p, (s + k) % seqs) for k in range(1, seqs)]
    )
    send, share, finish, drain = sum_over_feat(p, s, part, landed, shared, rs_send, rs_recv, ag_send, ag_recv)
    send()

    def at(ref, c):
        return ref.at[pl.ds(c * slab, slab), :]

    first = [remote(at(terms.at[1], c), at(rx1, c), x1s.at[c], x1r.at[c], back, s) for c in range(feats)]
    second = [remote(at(mid, c), at(rx2, c), x2s.at[c], x2r.at[c], side, s) for c in range(feats)]
    across = [remote(at(terms.at[3], c), at(rz, c), zs.at[c], zr.at[c], up, s) for c in range(feats)]
    for c in range(feats):
        first[c].start()
        across[c].start()

    slots = [(dy, h) for dy in (2, 1, 3, 0) for h in (0, 1)]

    def rows_of(dy, h, core_):
        there = half if h == 1 else 1 - half
        return pl.ds(pl.multiple_of(seq_at(there, (y + dy) % 4, core_) * piece, 32), piece)

    sibling = seq_at(half, y, 1 - core)
    up_y, down_y = seq_at(half, (y + 1) % 4, core), seq_at(half, (y + 3) % 4, core)
    other_half = seq_at(1 - half, y, core)
    cores = [
        remote(grads.at[rows_of(dy, h, 1 - core), :], crecv.at[i], cs.at[i], cr.at[i], p, sibling)
        for i, (dy, h) in enumerate(slots)
    ]
    for copy in cores:
        copy.start()
    far = [
        remote(q.at[0], ry2.at[0], y2s.at[0], y2r.at[0], p, up_y),
        remote(q.at[1], ry2.at[1], y2s.at[1], y2r.at[1], p, down_y),
    ]
    near = [remote(q.at[2 + i], ry1.at[i], y1s.at[i], y1r.at[i], p, up_y if i < 2 else down_y) for i in range(4)]

    def pair_sum(i):
        dy, h = slots[i]
        cores[i].wait_recv()
        q[i] = (grads[rows_of(dy, h, core), :].astype(F32) + crecv[i].astype(F32)).astype(BF16)

    share()
    for i in range(2):
        pair_sum(i)
        far[i].start()
    for i in range(2, 6):
        pair_sum(i)
    near[1].start()
    near[2].start()
    finish()
    for c in range(feats):
        backv[c * slab : (c + 1) * slab, :] = shared[c]
    product = lax.dot_general(tok[...], backv[...], (((0,), (0,)), ((), ())), preferred_element_type=F32) * norm_scale
    grow = gright.shape[0]
    for k in range(seqs):
        grsend[k] = product[k * grow : (k + 1) * grow, :].astype(BF16)
    rights = [
        remote(grsend.at[(s + k) % seqs], grrecv.at[k - 1], gs.at[k - 1], gr.at[k - 1], p, (s + k) % seqs)
        for k in range(1, seqs)
    ]
    for copy in rights:
        copy.start()

    def relay(c):
        first[c].wait_recv()
        here = slice(c * slab, (c + 1) * slab)
        mid[here, :] = (terms[2, here, :].astype(F32) + rx1[here, :].astype(F32)).astype(BF16)
        second[c].start()

    for c in range(4):
        relay(c)
    far[0].wait_recv()
    q[2] = (q[2].astype(F32) + ry2[0].astype(F32)).astype(BF16)
    near[0].start()
    far[1].wait_recv()
    q[5] = (q[5].astype(F32) + ry2[1].astype(F32)).astype(BF16)
    near[3].start()
    for i in range(6, 8):
        pair_sum(i)
    for c in range(4, feats):
        relay(c)
    low[...] = lax.dot_general(backv[...], right[...], (((1,), (1,)), ((), ())), preferred_element_type=F32)
    for c in range(feats):
        here = slice(c * slab, (c + 1) * slab)
        second[c].wait_recv()
        across[c].wait_recv()
        fin[c] = (
            low[here, :]
            + terms[0, here, :].astype(F32)
            + rx2[here, :].astype(F32)
            + rz[here, :].astype(F32)
        ).astype(BF16)
    spread = [
        remote(fin.at[(p + k) % feats], a2a.at[p], as_.at[k - 1], ar.at[k - 1], (p + k) % feats, s)
        for k in range(1, feats)
    ]
    for copy in spread:
        copy.start()
    a2a[p] = fin[p]
    for copy in near:
        copy.wait_recv()
    zsend[...] = (q[6].astype(F32) + ry1[0].astype(F32) + ry1[2].astype(F32)).astype(BF16)
    cross = remote(zsend, zrecv, hs, hr, p, other_half)
    cross.start()
    total = grsend[s].astype(F32)
    for k, copy in enumerate(rights):
        copy.wait_recv()
        total = total + grrecv[k].astype(F32)
    gright[...] = total
    for copy in spread:
        copy.wait_recv()
    for c in range(feats):
        gin[:, c * a2a.shape[2] : (c + 1) * a2a.shape[2]] = a2a[c]
    cross.wait_recv()
    mine = q[7].astype(F32) + ry1[1].astype(F32) + ry1[3].astype(F32) + zrecv[...].astype(F32)
    gblocks[...] = mine[:, :wide]
    gleft[...] = mine[:, wide:]
    drain()
    for copy in first + second + across + cores + far + near + rights + spread + [cross]:
        copy.wait_send()


def gather(terms, part, right, tokens, grads, norm_scale):
    rows, width = tokens.shape
    rank = right.shape[1]
    feats, seqs = lax.axis_size("feat"), lax.axis_size("seq")
    slab = rows // feats
    out_rows, wide_all = grads.shape
    piece = out_rows // seqs
    grow = width // seqs
    vmem_spec = pl.BlockSpec(memory_space=pltpu.VMEM)
    dma = pltpu.SemaphoreType.DMA
    f1, s1 = dma((feats - 1,)), dma((seqs - 1,))
    return pl.pallas_call(
        functools.partial(gather_kernel, norm_scale),
        out_shape=(
            jax.ShapeDtypeStruct((slab, feats * width), BF16),
            jax.ShapeDtypeStruct((piece, wide_all - rank), F32),
            jax.ShapeDtypeStruct((piece, rank), F32),
            jax.ShapeDtypeStruct((grow, rank), F32),
        ),
        in_specs=[vmem_spec] * 5,
        out_specs=(vmem_spec,) * 4,
        scratch_shapes=[
            pltpu.VMEM((feats - 1, slab, rank), F32),
            pltpu.VMEM((feats, slab, rank), BF16),
            pltpu.VMEM((rows, rank), BF16),
            pltpu.VMEM((rows, width), F32),
            pltpu.VMEM((rows, width), BF16),
            pltpu.VMEM((rows, width), BF16),
            pltpu.VMEM((rows, width), BF16),
            pltpu.VMEM((rows, width), BF16),
            pltpu.VMEM((feats, slab, width), BF16),
            pltpu.VMEM((feats, slab, width), BF16),
            pltpu.VMEM((8, piece, wide_all), BF16),
            pltpu.VMEM((8, piece, wide_all), BF16),
            pltpu.VMEM((2, piece, wide_all), BF16),
            pltpu.VMEM((4, piece, wide_all), BF16),
            pltpu.VMEM((piece, wide_all), BF16),
            pltpu.VMEM((piece, wide_all), BF16),
            pltpu.VMEM((seqs, grow, rank), BF16),
            pltpu.VMEM((seqs - 1, grow, rank), BF16),
            f1, f1, f1, f1,
            dma((feats,)), dma((feats,)), dma((feats,)), dma((feats,)), dma((feats,)), dma((feats,)), f1, f1,
            dma((8,)), dma((8,)), dma((2,)), dma((2,)), dma((4,)), dma((4,)), dma, dma, s1, s1,
        ],
        compiler_params=pltpu.CompilerParams(collective_id=1, has_side_effects=True, vmem_limit_bytes=VMEM_LIMIT),
    )(terms, part.reshape(feats, slab, rank), right, tokens, grads)


def local(tokens, block_weights, left_factor, right_factor, pattern, cotangent):
    tok_rows, local_width = tokens.shape
    norm_scale = 1.0 / math.sqrt(tok_rows * lax.axis_size("seq"))
    lids = pattern[:, 0] % (local_width // BLK)
    x1, x2, x3, latent = exchange(tokens, right_factor)
    activated, terms, back_part, grads = block_rows(
        lids, tokens, x1, x2, x3, latent, block_weights, left_factor, cotangent, norm_scale
    )
    grad_input, grad_blocks, grad_left, grad_right = gather(
        terms, back_part, right_factor, tokens, grads, norm_scale
    )
    return activated, grad_input[None], grad_blocks, grad_left, grad_right


def solution(mesh):
    in_specs = (
        P("seq", "feat"),
        P("feat", None),
        P("feat", None),
        P("feat", None),
        P("feat", None),
        P("seq", "feat"),
    )
    out_specs = (
        P("seq", "feat"),
        P("seq", "feat", None),
        P(("feat", "seq"), None),
        P(("feat", "seq"), None),
        P(("feat", "seq"), None),
    )
    return jax.shard_map(local, mesh=mesh, in_specs=in_specs, out_specs=out_specs, check_vma=False)
```

time: 453 us -> 184 us (0.41)
  Pallas kernels: 0 us -> 174 us
  blocking collectives: 118 us -> 0 us
  local copies, waits for them, and re-layouts: 98.5 us -> 7.19 us
  other arithmetic: 79.8 us -> 1.2 us
  waiting for transfers between devices: 70.2 us -> 0 us
  matrix products: 61.3 us -> 0 us
  between operations: 13.9 us -> 0.65 us
  starting transfers between devices: 10.4 us -> 0 us
    pallas_call x0 -> x3, Pallas kernels: none -> 174 us  [the longest x1 89.6 us: gather(): pl.pallas_call(functools.partial(gather_kernel, norm_scale), out_shape=(j...]
    psum x2 -> x0, blocking collectives: 102 us -> none  [the longest x1 61.9 us: local(): latent = lax.psum(latent_part, 'feat').astype(jnp.bfloat16)]
    scatter-add x4 -> x0, other arithmetic: 69.8 us -> none  [local(): level_term = jnp.zeros((tok_rows, local_blocks, BLK), jnp.float32).at[:,...]
    dot_general x9 -> x0, matrix products: 61.3 us -> none  [the longest x1 17 us: local(): jnp.einsum('tfo,foli->tfli', grad_rows, weight_blocks, preferred_element_...]
    reduce_scatter x2 -> x0, waiting for transfers between devices: 48.5 us -> none  [the longest x1 48.5 us: local(): lax.psum_scatter(product, 'seq', scatter_dimension=0, tiled=True)]
    reshape x10 -> x0, local copies, waits for them, and re-layouts: 33.5 us -> none  [the longest x3 9.64 us: local(): level_term = level_term.reshape(tok_rows, local_width)]
    ppermute x6 -> x0, waiting for transfers between devices: 21.6 us -> none  [from_partner(): return lax.ppermute(value, axis, pairs)]
    squeeze x1 -> x0, local copies, waits for them, and re-layouts: 20.2 us -> none  [local(): spread[:, :, level, :]]
  transfers between devices with their start and end apart: 9 -> 0, of which waited for: 3 -> 0; matrix products, arithmetic and copies ran while one was open for 40% -> 0% of each run, Pallas kernels for 0% -> 0%
where the time goes in v1:
time: 184 us; the launch traced here: 183 us
  Pallas kernels  174 us (95%)
  local copies, waits for them, and re-layouts  7.19 us (4%)
    pallas_call x1, Pallas kernels, gather(): pl.pallas_call(functools.partial(gather_kernel, norm_scale), out_shape=(j...  89.6 us
    pallas_call x1, Pallas kernels, exchange(): pl.pallas_call(exchange_kernel, out_shape=(whole, whole, whole, jax.Shape...  44.6 us
    pallas_call x1, Pallas kernels, block_rows(): pl.pallas_call(functools.partial(rows_kernel, norm_scale), grid_spec=pltp...  39.7 us
    unnamed x4, local copies, waits for them, and re-layouts  7.19 us

profile of v1, /device:TPU:0, one launch (start us, length us, event | category | flops | bytes accessed | tf_op | source)
XLA Modules:
  0.0 183.0 jit_solution(17355913109489974091)
XLA Ops:
  0.6 1.2 and_select_fusion.lid_ref
  1.8 44.6 %shard_map.101 = (bf16[512,1024]{1,0:T(8,128)(2,1)}, bf16[512,1024]{1,0:T(8,128)(2,1)}, bf16[512,1024]{1,0:T(8,128)(2,1)}, bf16[512,256]{1,0:T(8,128)(2,1)}) custom-call(bf16[512,1024]{1,0:T(8,128)(2,1)} %tok.5, bf16[1024,256]{1,0:T(8,128)(2,1)} %right.3), custom_call_target="tpu_custom_call" | custom-call | tf_op jit(solution)/shard_map/pallas_call | solution.py:131
  46.5 39.7 %shard_map.102 = (bf16[512,3584]{1,0:T(8,128)(2,1)}, bf16[4,512,1024]{2,1,0:T(8,128)(2,1)}, f32[512,256]{1,0:T(8,128)}, bf16[3584,768]{1,0:T(8,128)(2,1)}) custom-call(s32[28]{0:T(128)} %and_select_fusion.lid_ref, bf16[512,1024]{1,0:T(8,128)(2,1)} %tok.5, bf16[512,1024]{1,0:T(8,128)(2,1)} %get-tuple-element.17.x1, bf16[512,1024]{1,0:T(8,128)(2,1)} %get-tuple-element.18.x2, ...), custom_call_target="tpu_custom_call" | custom-call | tf_op jit(solution)/shard_map/pallas_call | solution.py:189
  86.2 89.6 %shard_map.103 = (bf16[64,8192]{1,0:T(8,128)(2,1)}, f32[224,512]{1,0:T(8,128)}, f32[224,256]{1,0:T(8,128)}, f32[64,256]{1,0:T(8,128)}) custom-call(bf16[4,512,1024]{2,1,0:T(8,128)(2,1)} %get-tuple-element.22.terms, f32[8,64,256]{2,1,0:T(8,128)} %bitcast.5, bf16[1024,256]{1,0:T(8,128)(2,1)} %right.3, bf16[512,1024]{1,0:T(8,128)(2,1)} %tok.5, ...), custom_call_target="tpu_custom_call" | custom-call | tf_op jit(solution)/shard_map/pallas_call | solution.py:371
  175.8 2.3 %copy.15 = bf16[1,64,8192]{2,1,0:T(8,128)(2,1)} copy(bf16[1,64,8192]{2,1,0:T(8,128)(2,1)} %bitcast.4) | data formatting | bytes 2097152
  178.1 1.8 copy.16
  179.9 1.6 copy.17
  181.5 1.5 copy.18

commit v2 on v0

v2 whole, which is shorter than its diff:
```python
import functools
import math

import jax
import jax.numpy as jnp
from jax import lax
from jax.experimental import pallas as pl
from jax.experimental.pallas import tpu as pltpu
from jax.sharding import PartitionSpec as P

BLK = 128
LEVELS = 4
FEATS = 8
SEQS = 16
UNROLL = 4
MESH = pl.DeviceIdType.MESH
F32 = jnp.float32
BF16 = jnp.bfloat16
VMEM_LIMIT = 67043328


def remote(src, dst, send_sem, recv_sem, feat, seq):
    return pltpu.make_async_remote_copy(
        src_ref=src,
        dst_ref=dst,
        send_sem=send_sem,
        recv_sem=recv_sem,
        device_id=(feat, seq),
        device_id_type=MESH,
    )


def greet(devices):
    barrier = pltpu.get_barrier_semaphore()
    for feat, seq in devices:
        pl.semaphore_signal(barrier, inc=1, device_id=(feat, seq), device_id_type=MESH)
    pl.semaphore_wait(barrier, len(devices))


class FeatSum:
    def __init__(self, p, s, part, outgoing, landed, shared, sems):
        rs_send, rs_recv, ag_send, ag_recv = sems
        self.p, self.part, self.outgoing, self.landed, self.shared = p, part, outgoing, landed, shared
        self.rs, self.ag = [], []
        for k in range(1, FEATS):
            there = (p + k) % FEATS
            self.rs.append(
                remote(outgoing.at[there], landed.at[k - 1], rs_send.at[k - 1], rs_recv.at[k - 1], there, s)
            )
            self.ag.append(remote(shared.at[p], shared.at[p], ag_send.at[k - 1], ag_recv.at[k - 1], there, s))

    def send(self):
        self.outgoing[...] = self.part[...].astype(BF16)
        for copy in self.rs:
            copy.start()

    def share(self):
        total = self.part[self.p]
        for k, copy in enumerate(self.rs):
            copy.wait_recv()
            total = total + self.landed[k].astype(F32)
        self.shared[self.p] = total.astype(BF16)
        for copy in self.ag:
            copy.start()

    def finish(self):
        for copy in self.ag:
            copy.wait_recv()

    def drain(self):
        for copy in self.rs + self.ag:
            copy.wait_send()


def loop(first, count, fn):
    def body(i, carry):
        for u in range(UNROLL):
            fn(first + i * UNROLL + u)
        return carry

    lax.fori_loop(0, count // UNROLL, body, 0)
    for u in range(count % UNROLL):
        fn(first + count - count % UNROLL + u)


def block_of(f):
    start = f * BLK
    return pl.ds(start if isinstance(start, int) else pl.multiple_of(start, BLK), BLK)


def kernel(norm_scale, *refs):
    (links, tok, w_hbm, left_hbm, cot_hbm, right) = refs[:6]
    (act_hbm, a2a, grad, gright) = refs[6:10]
    (
        xall, tokv, x1a, x1b, x2a, x2b, x3a, x3b, wv, leftv, gp, actv, sums, terms, grads,
        part, outgoing, landed, shared, lat, landed2, shared2, backv, rx1, rx2, rz,
        crecv, q, ry2, ry1, zsend, zrecv, grsend, grrecv,
    ) = refs[10:44]
    (
        lsem, x_send, x_recv, f_send, f_recv, z_send, z_recv, rs_send, rs_recv, ag_send, ag_recv,
        rs_send2, rs_recv2, ag_send2, ag_recv2, x1s, x1r, x2s, x2r, zs, zr, as_, ar,
        cs, cr, y2s, y2r, y1s, y1r, hs, hr, gs, gr, act_sem,
    ) = refs[44:]
    p, s = lax.axis_index("feat"), lax.axis_index("seq")
    x, z = p // 2, p % 2
    side, back, up = 2 * (x + 1 - 2 * (x % 2)) + z, 2 * (3 - x) + z, 2 * x + 1 - z
    core, y, half = s % 2, (s // 2) % 4, s // 8
    slab, rank = part.shape[1], part.shape[2]
    rows, width = tokv.shape
    mid_rows = rows // 2
    blocks = width // BLK
    row_blocks = wv.shape[0] // BLK
    wide = LEVELS * BLK
    piece = q.shape[1]

    loads = [
        pltpu.make_async_copy(src, dst, lsem.at[i])
        for i, (src, dst) in enumerate([(tok, tokv), (w_hbm, wv), (left_hbm, leftv), (cot_hbm, gp)])
    ]
    for copy in loads:
        copy.start()
    greet([((p + k) % FEATS, s) for k in range(1, FEATS)] + [(p, (s + k) % SEQS) for k in range(1, SEQS)])

    def chunk(pair, c):
        return pair[c // 4].at[pl.ds((c % 4) * slab, slab), :]

    def at(ref, c):
        return ref.at[pl.ds(c * slab, slab), :]

    own = [remote(at(tok, c), chunk((x2a, x2b), c), x_send.at[c], x_recv.at[c], side, s) for c in range(FEATS)]
    passed = [
        remote(chunk((x2a, x2b), c), chunk((x1a, x1b), c), f_send.at[c], f_recv.at[c], back, s) for c in range(FEATS)
    ]
    across = [remote(at(tok, c), chunk((x3a, x3b), c), z_send.at[c], z_recv.at[c], up, s) for c in range(FEATS)]
    latent = FeatSum(p, s, part, outgoing, landed, shared, (rs_send, rs_recv, ag_send, ag_recv))
    own[0].start()
    across[0].start()
    loads[0].wait()
    for c in range(FEATS):
        part[c] = jnp.dot(tokv[c * slab : (c + 1) * slab, :], right[...], preferred_element_type=F32)
    latent.send()
    for c in (1, 2):
        own[c].start()
        across[c].start()

    sums[row_blocks] = jnp.zeros(sums.shape[1:], F32)

    def relay(c):
        own[c].wait_recv()
        passed[c].start()
        if c + 3 < FEATS:
            own[c + 3].start()
            across[c + 3].start()

    relay(0)
    latent.share()
    for c in range(1, 5):
        relay(c)

    def halves(h):
        return slice(h * mid_rows, (h + 1) * mid_rows)

    def repack(h):
        for j, source in enumerate((tokv.at[halves(h), :], (x1a, x1b)[h], (x2a, x2b)[h], (x3a, x3b)[h])):
            for b in range(blocks):
                xall[b, halves(h), j * BLK : (j + 1) * BLK] = source[:, b * BLK : (b + 1) * BLK]

    def picked(here, f):
        return jnp.concatenate([xall[links[row_blocks + blocks + f], here, :], lat[here, :]], axis=1)

    curve = math.sqrt(2.0 / math.pi)

    def forward(h, first, count):
        here = slice(h * mid_rows, (h + 1) * mid_rows)

        def one(f):
            fr = block_of(f)
            wl = jnp.concatenate([wv[fr, :], leftv[fr, :]], axis=1)
            pre = lax.dot_general(picked(halves(h), f), wl, (((1,), (1,)), ((), ())), preferred_element_type=F32)
            square = pre * pre
            th = jnp.tanh(curve * (pre + 0.044715 * (square * pre)))
            cdf = 0.5 + 0.5 * th
            actv[here, fr] = (pre * cdf).astype(BF16)
            slope = cdf + (0.5 * curve) * pre * (1.0 - th * th) * (1.0 + (3.0 * 0.044715) * square)
            gp[here, fr] = (gp[here, fr].astype(F32) * slope).astype(BF16)

        loop(first, count, one)

    def spread(h):
        here = slice(h * mid_rows, (h + 1) * mid_rows)

        def one(f):
            fr = block_of(f)
            sums[f] = sums[links[f]] + jnp.dot(gp[here, fr], wv[fr, :], preferred_element_type=F32)

        loop(0, row_blocks, one)
        for b in range(blocks):
            total = sums[links[row_blocks + b]].astype(BF16)
            for j in range(LEVELS):
                terms[j, here, b * BLK : (b + 1) * BLK] = total[:, j * BLK : (j + 1) * BLK]

    first = [remote(at(terms.at[1], c), at(rx1, c), x1s.at[c], x1r.at[c], back, s) for c in range(FEATS)]
    second = [remote(at(rx1, c), at(rx2, c), x2s.at[c], x2r.at[c], side, s) for c in range(FEATS)]
    upward = [remote(at(terms.at[3], c), at(rz, c), zs.at[c], zr.at[c], up, s) for c in range(FEATS)]

    def send_terms(c):
        first[c].start()
        upward[c].start()

    def hand_on(c):
        here = slice(c * slab, (c + 1) * slab)
        first[c].wait_recv()
        rx1[here, :] = (terms[2, here, :].astype(F32) + rx1[here, :].astype(F32)).astype(BF16)
        second[c].start()

    latent.finish()
    for c in range(FEATS):
        lat[c * slab : (c + 1) * slab, :] = shared[c]
    for c in range(4):
        passed[c].wait_recv()
        across[c].wait_recv()
    for copy in loads[1:]:
        copy.wait()
    repack(0)
    forward(0, 0, 8)
    relay(5)
    forward(0, 8, 8)
    relay(6)
    forward(0, 16, 8)
    relay(7)
    forward(0, 24, row_blocks - 24)
    spread(0)
    for c in range(4):
        own[4 + c].wait_send()
        send_terms(c)
    for c in range(4, FEATS):
        passed[c].wait_recv()
        across[c].wait_recv()
    repack(1)
    forward(1, 0, 16)
    hand_on(0)
    forward(1, 16, row_blocks - 16)
    hand_on(1)
    act_out = pltpu.make_async_copy(actv, act_hbm, act_sem)
    act_out.start()
    for c in range(FEATS):
        part[c] = jnp.dot(gp[c * slab : (c + 1) * slab, :], leftv[...], preferred_element_type=F32)
    latent.drain()
    back_sum = FeatSum(p, s, part, outgoing, landed2, shared2, (rs_send2, rs_recv2, ag_send2, ag_recv2))
    back_sum.send()

    def seq_at(half_, y_, core_):
        return half_ * 8 + y_ * 2 + core_

    def grad_rows(first_block, count):
        def one(f):
            fr = block_of(f)
            xl = picked(slice(0, rows), f)
            grads[fr, :] = (
                lax.dot_general(gp[:, fr], xl, (((0,), (0,)), ((), ())), preferred_element_type=F32) * norm_scale
            ).astype(BF16)

        loop(first_block, count, one)

    slots = [(dy, h) for dy in (2, 1, 3, 0) for h in (0, 1)]

    def rows_of(dy, h, core_):
        there = half if h == 1 else 1 - half
        return pl.ds(pl.multiple_of(seq_at(there, (y + dy) % 4, core_) * piece, 32), piece)

    sibling = seq_at(half, y, 1 - core)
    up_y, down_y = seq_at(half, (y + 1) % 4, core), seq_at(half, (y + 3) % 4, core)
    other_half = seq_at(1 - half, y, core)
    cores = [
        remote(grads.at[rows_of(dy, h, 1 - core), :], crecv.at[i], cs.at[i], cr.at[i], p, sibling)
        for i, (dy, h) in enumerate(slots)
    ]
    far = [
        remote(q.at[0], ry2.at[0], y2s.at[0], y2r.at[0], p, up_y),
        remote(q.at[1], ry2.at[1], y2s.at[1], y2r.at[1], p, down_y),
    ]
    near = [remote(q.at[2 + i], ry1.at[i], y1s.at[i], y1r.at[i], p, up_y if i < 2 else down_y) for i in range(4)]

    def pair_sum(i):
        dy, h = slots[i]
        cores[i].wait_recv()
        q[i] = (grads[rows_of(dy, h, core), :].astype(F32) + crecv[i].astype(F32)).astype(BF16)

    far_pair = ((y + 2) % 4) // 2
    per_pair = row_blocks // 4
    for h in (0, 1):
        grad_rows(far_pair * per_pair + h * 2 * per_pair, per_pair)
    cores[0].start()
    cores[1].start()
    hand_on(2)
    hand_on(3)
    spread(1)
    for c in (4, 5, 6):
        send_terms(c)
    for i in range(2):
        pair_sum(i)
        far[i].start()
    back_sum.share()
    for h in (0, 1):
        grad_rows((1 - far_pair) * per_pair + h * 2 * per_pair, per_pair)
    for copy in cores[2:]:
        copy.start()
    send_terms(7)
    pair_sum(3)
    near[1].start()
    pair_sum(4)
    near[2].start()
    hand_on(4)
    pair_sum(2)
    pair_sum(5)
    back_sum.finish()
    for c in range(FEATS):
        backv[c * slab : (c + 1) * slab, :] = shared2[c]
    product = lax.dot_general(tokv[...], backv[...], (((0,), (0,)), ((), ())), preferred_element_type=F32) * norm_scale
    grow = gright.shape[0]
    for k in range(SEQS):
        grsend[k] = product[k * grow : (k + 1) * grow, :].astype(BF16)
    rights = [
        remote(grsend.at[(s + k) % SEQS], grrecv.at[k - 1], gs.at[k - 1], gr.at[k - 1], p, (s + k) % SEQS)
        for k in range(1, SEQS)
    ]
    for copy in rights:
        copy.start()
    hand_on(5)
    far[0].wait_recv()
    q[2] = (q[2].astype(F32) + ry2[0].astype(F32)).astype(BF16)
    near[0].start()
    far[1].wait_recv()
    q[5] = (q[5].astype(F32) + ry2[1].astype(F32)).astype(BF16)
    near[3].start()
    hand_on(6)
    hand_on(7)
    pair_sum(6)
    pair_sum(7)
    for c in range(FEATS):
        here = slice(c * slab, (c + 1) * slab)
        low = lax.dot_general(backv[here, :], right[...], (((1,), (1,)), ((), ())), preferred_element_type=F32)
        second[c].wait_recv()
        upward[c].wait_recv()
        terms[0, here, :] = (
            low + terms[0, here, :].astype(F32) + rx2[here, :].astype(F32) + rz[here, :].astype(F32)
        ).astype(BF16)
    regroup = []
    for k in range(1, FEATS):
        there = (p + k) % FEATS
        mine_rows = pl.ds(pl.multiple_of(there * slab, slab), slab)
        regroup.append(
            remote(terms.at[0, mine_rows, :], a2a.at[p], as_.at[k - 1], ar.at[k - 1], there, s)
        )
    for copy in regroup:
        copy.start()
    a2a[p] = terms[0, pl.ds(pl.multiple_of(p * slab, slab), slab), :]
    for copy in near:
        copy.wait_recv()
    zsend[...] = (q[6].astype(F32) + ry1[0].astype(F32) + ry1[2].astype(F32)).astype(BF16)
    cross = remote(zsend, zrecv, hs, hr, p, other_half)
    cross.start()
    total = grsend[s].astype(F32)
    for k, copy in enumerate(rights):
        copy.wait_recv()
        total = total + grrecv[k].astype(F32)
    gright[...] = total
    cross.wait_recv()
    grad[...] = q[7].astype(F32) + ry1[1].astype(F32) + ry1[3].astype(F32) + zrecv[...].astype(F32)
    for copy in regroup:
        copy.wait_recv()
    back_sum.drain()
    for copy in own[:4] + passed + across + first + second + upward + cores + far + near + rights + regroup + [cross]:
        copy.wait_send()
    act_out.wait()


def chain_links(pattern, blocks):
    count = pattern.shape[0]
    places = pattern[:, 0] % blocks
    rows = jnp.arange(count)
    wanted = jnp.concatenate([places, jnp.arange(blocks, dtype=places.dtype)])
    limit = jnp.concatenate([rows, jnp.full((blocks,), count)])
    found = (wanted[:, None] == places[None, :]) & (rows[None, :] < limit[:, None])
    latest = jnp.max(jnp.where(found, rows[None, :], -1), axis=1)
    return jnp.concatenate([jnp.where(latest < 0, count, latest), places]).astype(jnp.int32)


def fused(tokens, weights, left, right, pattern, cotangent, norm_scale):
    rows, width = tokens.shape
    out_rows, wide = weights.shape
    rank = left.shape[1]
    slab = rows // FEATS
    row_blocks, blocks = out_rows // BLK, width // BLK
    piece, grow = out_rows // SEQS, width // SEQS
    all_wide = wide + rank
    any_spec = pl.BlockSpec(memory_space=pl.ANY)
    vmem_spec = pl.BlockSpec(memory_space=pltpu.VMEM)
    smem_spec = pl.BlockSpec(memory_space=pltpu.SMEM)
    dma = pltpu.SemaphoreType.DMA
    d8, d7, d4, d2, d15 = dma((8,)), dma((7,)), dma((4,)), dma((2,)), dma((15,))
    half = pltpu.VMEM((rows // 2, width), BF16)
    whole = pltpu.VMEM((rows, width), BF16)
    slabs, slabs7 = pltpu.VMEM((FEATS, slab, rank), BF16), pltpu.VMEM((FEATS - 1, slab, rank), BF16)
    flat = pltpu.VMEM((rows, rank), BF16)
    return pl.pallas_call(
        functools.partial(kernel, norm_scale),
        out_shape=(
            jax.ShapeDtypeStruct((rows, out_rows), BF16),
            jax.ShapeDtypeStruct((FEATS, slab, width), BF16),
            jax.ShapeDtypeStruct((piece, all_wide), F32),
            jax.ShapeDtypeStruct((grow, rank), F32),
        ),
        in_specs=[smem_spec, any_spec, any_spec, any_spec, any_spec, vmem_spec],
        out_specs=(any_spec, vmem_spec, vmem_spec, vmem_spec),
        scratch_shapes=[
            pltpu.VMEM((blocks, rows, wide), BF16),
            whole, half, half, half, half, half, half,
            pltpu.VMEM((out_rows, wide), BF16), pltpu.VMEM((out_rows, rank), BF16),
            pltpu.VMEM((rows, out_rows), BF16), pltpu.VMEM((rows, out_rows), BF16),
            pltpu.VMEM((row_blocks + 1, rows // 2, wide), F32),
            pltpu.VMEM((LEVELS, rows, width), BF16),
            pltpu.VMEM((out_rows, all_wide), BF16),
            pltpu.VMEM((FEATS, slab, rank), F32), slabs, slabs7, slabs, flat, slabs7, slabs, flat,
            whole, whole, whole,
            pltpu.VMEM((8, piece, all_wide), BF16), pltpu.VMEM((8, piece, all_wide), BF16),
            pltpu.VMEM((2, piece, all_wide), BF16), pltpu.VMEM((4, piece, all_wide), BF16),
            pltpu.VMEM((piece, all_wide), BF16), pltpu.VMEM((piece, all_wide), BF16),
            pltpu.VMEM((SEQS, grow, rank), BF16), pltpu.VMEM((SEQS - 1, grow, rank), BF16),
            d4, d8, d8, d8, d8, d8, d8, d7, d7, d7, d7, d7, d7, d7, d7,
            d8, d8, d8, d8, d8, d8, d7, d7, d8, d8, d2, d2, d4, d4, dma, dma, d15, d15, dma,
        ],
        compiler_params=pltpu.CompilerParams(collective_id=0, has_side_effects=True, vmem_limit_bytes=VMEM_LIMIT),
    )(chain_links(pattern, blocks), tokens, weights, left, cotangent, right)


def place_kernel(wide, act, a2a, grad, gright, act_o, gin_o, gb_o, gl_o, gr_o, actv, a2av, gradv, grv, in_sem, out_sem):
    parts = 4
    step = act.shape[0] // parts
    width = a2a.shape[2]
    rows = [pl.ds(i * step, step) for i in range(parts)]
    moves = [(act.at[r, :], actv.at[r, :], [(actv.at[r, :], act_o.at[r, :])]) for r in rows]
    moves.append(
        (grad, gradv, [(gradv.at[:, pl.ds(0, wide)], gb_o), (gradv.at[:, pl.ds(wide, gradv.shape[1] - wide)], gl_o)])
    )
    moves.append((gright, grv, [(grv, gr_o)]))
    moves += [
        (a2a.at[c], a2av.at[c], [(a2av.at[c], gin_o.at[:, pl.ds(c * width, width)])]) for c in range(a2a.shape[0])
    ]
    ins = [pltpu.make_async_copy(src, mid, in_sem.at[i]) for i, (src, mid, _) in enumerate(moves)]
    for copy in ins:
        copy.start()
    outs = []
    for copy, (_, _, after) in zip(ins, moves):
        copy.wait()
        for src, dst in after:
            outs.append(pltpu.make_async_copy(src, dst, out_sem.at[len(outs)]))
            outs[-1].start()
    for copy in outs:
        copy.wait()


def place(act, a2a, grad, gright, wide):
    any_spec = pl.BlockSpec(memory_space=pl.ANY)
    feats, slab, width = a2a.shape
    piece, all_wide = grad.shape
    dma = pltpu.SemaphoreType.DMA
    return pl.pallas_call(
        functools.partial(place_kernel, wide),
        out_shape=(
            jax.ShapeDtypeStruct(act.shape, BF16),
            jax.ShapeDtypeStruct((slab, feats * width), BF16),
            jax.ShapeDtypeStruct((piece, wide), F32),
            jax.ShapeDtypeStruct((piece, all_wide - wide), F32),
            jax.ShapeDtypeStruct(gright.shape, F32),
        ),
        in_specs=[any_spec] * 4,
        out_specs=(any_spec,) * 5,
        scratch_shapes=[
            pltpu.VMEM(act.shape, BF16), pltpu.VMEM(a2a.shape, BF16),
            pltpu.VMEM(grad.shape, F32), pltpu.VMEM(gright.shape, F32),
            dma((14,)), dma((15,)),
        ],
        compiler_params=pltpu.CompilerParams(vmem_limit_bytes=16 * 1024 * 1024),
    )(act, a2a, grad, gright)


def local(tokens, block_weights, left_factor, right_factor, pattern, cotangent):
    norm_scale = 1.0 / math.sqrt(tokens.shape[0] * lax.axis_size("seq"))
    act, a2a, grad, gright = fused(
        tokens, block_weights, left_factor, right_factor, pattern, cotangent, norm_scale
    )
    activated, grad_input, grad_blocks, grad_left, grad_right = place(act, a2a, grad, gright, block_weights.shape[1])
    return activated, grad_input[None], grad_blocks, grad_left, grad_right


def solution(mesh):
    in_specs = (
        P("seq", "feat"),
        P("feat", None),
        P("feat", None),
        P("feat", None),
        P("feat", None),
        P("seq", "feat"),
    )
    out_specs = (
        P("seq", "feat"),
        P("seq", "feat", None),
        P(("feat", "seq"), None),
        P(("feat", "seq"), None),
        P(("feat", "seq"), None),
    )
    return jax.shard_map(local, mesh=mesh, in_specs=in_specs, out_specs=out_specs, check_vma=False)
```

time: 453 us -> 121 us (0.27)
  blocking collectives: 118 us -> 0 us
  Pallas kernels: 0 us -> 112 us
  local copies, waits for them, and re-layouts: 98.5 us -> 5.2 us
  other arithmetic: 79.8 us -> 2.1 us
  waiting for transfers between devices: 70.2 us -> 0 us
  matrix products: 61.3 us -> 0 us
  between operations: 13.9 us -> 0.82 us
  starting transfers between devices: 10.4 us -> 0 us
    pallas_call x0 -> x2, Pallas kernels: none -> 112 us  [the longest x1 107 us: fused(): pl.pallas_call(functools.partial(kernel, norm_scale), out_shape=(jax.Shap...]
    psum x2 -> x0, blocking collectives: 102 us -> none  [the longest x1 61.9 us: local(): latent = lax.psum(latent_part, 'feat').astype(jnp.bfloat16)]
    scatter-add x4 -> x0, other arithmetic: 69.8 us -> none  [local(): level_term = jnp.zeros((tok_rows, local_blocks, BLK), jnp.float32).at[:,...]
    dot_general x9 -> x0, matrix products: 61.3 us -> none  [the longest x1 17 us: local(): jnp.einsum('tfo,foli->tfli', grad_rows, weight_blocks, preferred_element_...]
    reduce_scatter x2 -> x0, waiting for transfers between devices: 48.5 us -> none  [the longest x1 48.5 us: local(): lax.psum_scatter(product, 'seq', scatter_dimension=0, tiled=True)]
    reshape x10 -> x0, local copies, waits for them, and re-layouts: 33.5 us -> none  [the longest x3 9.64 us: local(): level_term = level_term.reshape(tok_rows, local_width)]
    ppermute x6 -> x0, waiting for transfers between devices: 21.6 us -> none  [from_partner(): return lax.ppermute(value, axis, pairs)]
    squeeze x1 -> x0, local copies, waits for them, and re-layouts: 20.2 us -> none  [local(): spread[:, :, level, :]]
  transfers between devices with their start and end apart: 9 -> 0, of which waited for: 3 -> 0; matrix products, arithmetic and copies ran while one was open for 40% -> 0% of each run, Pallas kernels for 0% -> 0%
where the time goes in v2:
time: 121 us; the launch traced here: 120 us
  Pallas kernels  112 us (93%)
  local copies, waits for them, and re-layouts  5.2 us (4%)
  other arithmetic  2.1 us (2%)
    pallas_call x1, Pallas kernels, fused(): pl.pallas_call(functools.partial(kernel, norm_scale), out_shape=(jax.Shap...  107 us
    pallas_call x1, Pallas kernels, place(): pl.pallas_call(functools.partial(place_kernel, wide), out_shape=(jax.Shap...  5.2 us
    unnamed x8, local copies, waits for them, and re-layouts  5.19 us

profile of v2, /device:TPU:0, one launch (start us, length us, event | category | flops | bytes accessed | tf_op | source)
XLA Modules:
  0.0 120.5 jit_solution(8318623877611502911)
XLA Ops:
  0.6 0.7 and_select_fusion
  1.3 0.1 pad_add_fusion
  1.4 0.7 select_reduce_fusion
  2.2 0.6 pad_add_fusion.1.refs_0_
  2.7 107.2 %shard_map.101 = (bf16[512,3584]{1,0:T(8,128)(2,1)}, bf16[8,64,1024]{2,1,0:T(8,128)(2,1)}, f32[224,768]{1,0:T(8,128)}, f32[64,256]{1,0:T(8,128)}) custom-call(s32[64]{0:T(128)} %pad_add_fusion.1.refs_0_, bf16[512,1024]{1,0:T(8,128)(2,1)} %refs_1_.1, bf16[3584,512]{1,0:T(8,128)(2,1)} %refs_2_.1, bf16[3584,256]{1,0:T(8,128)(2,1)} %refs_3_.1, ...), custom_call_target="tpu_custom_call" | custom-call | tf_op jit(solution)/shard_map/pallas_call | solution.py:406
  109.9 0.0 copy-start
  109.9 2.0 %copy-done = bf16[512,3584]{1,0:T(8,128)(2,1)S(1)} copy-done((bf16[512,3584]{1,0:T(8,128)(2,1)S(1)}, bf16[512,3584]{1,0:T(8,128)(2,1)}, u32[]{:S(2)}) %copy-start) | copy-done | bytes 3670040
  112.0 0.0 copy-start.1
  112.0 1.2 %copy-done.1 = bf16[8,64,1024]{2,1,0:T(8,128)(2,1)S(1)} copy-done((bf16[8,64,1024]{2,1,0:T(8,128)(2,1)S(1)}, bf16[8,64,1024]{2,1,0:T(8,128)(2,1)}, u32[]{:S(2)}) %copy-start.1) | copy-done | bytes 1048600
  113.2 0.0 copy-start.2
  113.2 1.1 copy-done.2
  114.3 0.0 copy-start.3
  114.3 0.8 copy-done.3
  115.1 5.2 %shard_map.102 = (bf16[512,3584]{1,0:T(8,128)(2,1)}, bf16[64,8192]{1,0:T(8,128)(2,1)}, f32[224,512]{1,0:T(8,128)}, f32[224,256]{1,0:T(8,128)}, f32[64,256]{1,0:T(8,128)}) custom-call(bf16[512,3584]{1,0:T(8,128)(2,1)S(1)} %copy-done, bf16[8,64,1024]{2,1,0:T(8,128)(2,1)S(1)} %copy-done.1, f32[224,768]{1,0:T(8,128)S(1)} %copy-done.2, f32[64,256]{1,0:T(8,128)S(1)} %copy-done.3), custom_call_target="tpu_custom_call" | custom-call | tf_op jit(solution)/shard_map/pallas_call | solution.py:468
  (2 shorter events, 0.0 us)
Async XLA Ops:
  109.9 2.0 %copy-start = (bf16[512,3584]{1,0:T(8,128)(2,1)S(1)}, bf16[512,3584]{1,0:T(8,128)(2,1)}, u32[]{:S(2)}) copy-start(bf16[512,3584]{1,0:T(8,128)(2,1)} %get-tuple-element.14.act) | copy-start | bytes 11010052
  112.0 1.2 %copy-start.1 = (bf16[8,64,1024]{2,1,0:T(8,128)(2,1)S(1)}, bf16[8,64,1024]{2,1,0:T(8,128)(2,1)}, u32[]{:S(2)}) copy-start(bf16[8,64,1024]{2,1,0:T(8,128)(2,1)} %get-tuple-element.15.a2a) | copy-start | bytes 3145732
  113.2 1.1 copy-start.2
  114.3 0.8 copy-start.3

commit v3 on v2

--- a/solution.py
+++ b/solution.py
@@ -93,53 +93,65 @@
     (act_hbm, a2a, grad, gright) = refs[6:10]
     (
         xall, tokv, x1a, x1b, x2a, x2b, x3a, x3b, wv, leftv, gp, actv, sums, terms, grads,
-        part, outgoing, landed, shared, lat, landed2, shared2, backv, rx1, rx2, rz,
+        part, outgoing, landed, shared, lat, backp, backo, backl, backs, backv, rx1, rx2, rz,
         crecv, q, ry2, ry1, zsend, zrecv, grsend, grrecv,
-    ) = refs[10:44]
+    ) = refs[10:46]
     (
         lsem, x_send, x_recv, f_send, f_recv, z_send, z_recv, rs_send, rs_recv, ag_send, ag_recv,
         rs_send2, rs_recv2, ag_send2, ag_recv2, x1s, x1r, x2s, x2r, zs, zr, as_, ar,
         cs, cr, y2s, y2r, y1s, y1r, hs, hr, gs, gr, act_sem,
-    ) = refs[44:]
+    ) = refs[46:]
     p, s = lax.axis_index("feat"), lax.axis_index("seq")
     x, z = p // 2, p % 2
     side, back, up = 2 * (x + 1 - 2 * (x % 2)) + z, 2 * (3 - x) + z, 2 * x + 1 - z
     core, y, half = s % 2, (s // 2) % 4, s // 8
     slab, rank = part.shape[1], part.shape[2]
-    rows, width = tokv.shape
+    small, width = tokv.shape[2], tokv.shape[3]
+    rows = FEATS * slab
     mid_rows = rows // 2
     blocks = width // BLK
     row_blocks = wv.shape[0] // BLK
     wide = LEVELS * BLK
     piece = q.shape[1]
 
-    loads = [
-        pltpu.make_async_copy(src, dst, lsem.at[i])
-        for i, (src, dst) in enumerate([(tok, tokv), (w_hbm, wv), (left_hbm, leftv), (cot_hbm, gp)])
-    ]
-    for copy in loads:
+    def part_of(ref, h, c):
+        return ref.at[pl.ds(h * mid_rows + c * small, small), :]
+
+    tok_loads = [pltpu.make_async_copy(tok.at[:, h], tokv.at[h], lsem.at[h]) for h in range(2)]
+    loads = [pltpu.make_async_copy(w_hbm, wv, lsem.at[2]), pltpu.make_async_copy(left_hbm, leftv, lsem.at[3])]
+    for h in range(2):
+        for c in range(FEATS):
+            loads.append(
+                pltpu.make_async_copy(cot_hbm.at[c, h], part_of(gp, h, c), lsem.at[4 + h * FEATS + c])
+            )
+    for copy in tok_loads + loads:
         copy.start()
     greet([((p + k) % FEATS, s) for k in range(1, FEATS)] + [(p, (s + k) % SEQS) for k in range(1, SEQS)])
 
     def chunk(pair, c):
-        return pair[c // 4].at[pl.ds((c % 4) * slab, slab), :]
+        return pair[c // 4].at[pl.ds((c % 4) * 2, 2)]
+
+    def own_chunk(c):
+        return tok.at[pl.ds((c % 4) * 2, 2), c // 4]
 
     def at(ref, c):
         return ref.at[pl.ds(c * slab, slab), :]
 
-    own = [remote(at(tok, c), chunk((x2a, x2b), c), x_send.at[c], x_recv.at[c], side, s) for c in range(FEATS)]
+    own = [remote(own_chunk(c), chunk((x2a, x2b), c), x_send.at[c], x_recv.at[c], side, s) for c in range(FEATS)]
     passed = [
         remote(chunk((x2a, x2b), c), chunk((x1a, x1b), c), f_send.at[c], f_recv.at[c], back, s) for c in range(FEATS)
     ]
-    across = [remote(at(tok, c), chunk((x3a, x3b), c), z_send.at[c], z_recv.at[c], up, s) for c in range(FEATS)]
+    across = [remote(own_chunk(c), chunk((x3a, x3b), c), z_send.at[c], z_recv.at[c], up, s) for c in range(FEATS)]
     latent = FeatSum(p, s, part, outgoing, landed, shared, (rs_send, rs_recv, ag_send, ag_recv))
     own[0].start()
     across[0].start()
-    loads[0].wait()
+    for copy in tok_loads:
+        copy.wait()
     for c in range(FEATS):
-        part[c] = jnp.dot(tokv[c * slab : (c + 1) * slab, :], right[...], preferred_element_type=F32)
+        mine = tokv[c // 4, (c % 4) * 2 : (c % 4) * 2 + 2].reshape(slab, width)
+        part[c] = jnp.dot(mine, right[...], preferred_element_type=F32)
     latent.send()
-    for c in (1, 2):
+    for c in (1,):
         own[c].start()
         across[c].start()
 
@@ -148,9 +160,9 @@
     def relay(c):
         own[c].wait_recv()
         passed[c].start()
-        if c + 3 < FEATS:
-            own[c + 3].start()
-            across[c + 3].start()
+        if c + 2 < FEATS:
+            own[c + 2].start()
+            across[c + 2].start()
 
     relay(0)
     latent.share()
@@ -161,9 +173,10 @@
         return slice(h * mid_rows, (h + 1) * mid_rows)
 
     def repack(h):
-        for j, source in enumerate((tokv.at[halves(h), :], (x1a, x1b)[h], (x2a, x2b)[h], (x3a, x3b)[h])):
+        for j, source in enumerate((tokv.at[h], (x1a, x1b)[h], (x2a, x2b)[h], (x3a, x3b)[h])):
             for b in range(blocks):
-                xall[b, halves(h), j * BLK : (j + 1) * BLK] = source[:, b * BLK : (b + 1) * BLK]
+                block = source[:, :, b * BLK : (b + 1) * BLK].reshape(mid_rows, BLK)
+                xall[b, halves(h), j * BLK : (j + 1) * BLK] = block
 
     def picked(here, f):
         return jnp.concatenate([xall[links[row_blocks + blocks + f], here, :], lat[here, :]], axis=1)
@@ -186,14 +199,17 @@
 
         loop(first, count, one)
 
-    def spread(h):
+    def spread(h, begin, count):
         here = slice(h * mid_rows, (h + 1) * mid_rows)
 
         def one(f):
             fr = block_of(f)
             sums[f] = sums[links[f]] + jnp.dot(gp[here, fr], wv[fr, :], preferred_element_type=F32)
 
-        loop(0, row_blocks, one)
+        loop(begin, count, one)
+
+    def collect(h):
+        here = slice(h * mid_rows, (h + 1) * mid_rows)
         for b in range(blocks):
             total = sums[links[row_blocks + b]].astype(BF16)
             for j in range(LEVELS):
@@ -212,6 +228,51 @@
         first[c].wait_recv()
         rx1[here, :] = (terms[2, here, :].astype(F32) + rx1[here, :].astype(F32)).astype(BF16)
         second[c].start()
+
+    def back_sum_of(h):
+        return FeatSum(
+            p, s, backp.at[h], backo.at[h], backl.at[h], backs.at[h],
+            (rs_send2.at[h], rs_recv2.at[h], ag_send2.at[h], ag_recv2.at[h]),
+        )
+
+    back_sums = [back_sum_of(0), back_sum_of(1)]
+
+    def start_back(h):
+        for c in range(FEATS):
+            here = slice(h * mid_rows + c * small, h * mid_rows + (c + 1) * small)
+            if c % 4 == 0:
+                wider = slice(h * mid_rows + c * small, h * mid_rows + (c + 4) * small)
+                four = jnp.dot(gp[wider, :], leftv[...], preferred_element_type=F32)
+            backp[h, c] = four[(c % 4) * small : (c % 4 + 1) * small, :]
+        back_sums[h].send()
+
+    def end_back(h):
+        back_sums[h].finish()
+        for c in range(FEATS):
+            backv[h * mid_rows + c * small : h * mid_rows + (c + 1) * small, :] = backs[h, c]
+
+    regroup = []
+    for h in range(2):
+        for k in range(1, FEATS):
+            there = (p + k) % FEATS
+            src = terms.at[0, pl.ds(pl.multiple_of(h * mid_rows + there * small, small), small), :]
+            dst = a2a.at[p, pl.ds(h * small, small), :]
+            regroup.append(remote(src, dst, as_.at[h, k - 1], ar.at[h, k - 1], there, s))
+
+    def finish_half(h):
+        for c in range(h * 4, h * 4 + 4):
+            here = slice(c * slab, (c + 1) * slab)
+            low = lax.dot_general(backv[here, :], right[...], (((1,), (1,)), ((), ())), preferred_element_type=F32)
+            second[c].wait_recv()
+            upward[c].wait_recv()
+            terms[0, here, :] = (
+                low + terms[0, here, :].astype(F32) + rx2[here, :].astype(F32) + rz[here, :].astype(F32)
+            ).astype(BF16)
+        for copy in regroup[h * (FEATS - 1) : (h + 1) * (FEATS - 1)]:
+            copy.start()
+        a2a[p, h * small : (h + 1) * small, :] = terms[
+            0, pl.ds(pl.multiple_of(h * mid_rows + p * small, small), small), :
+        ]
 
     latent.finish()
     for c in range(FEATS):
@@ -219,7 +280,7 @@
     for c in range(4):
         passed[c].wait_recv()
         across[c].wait_recv()
-    for copy in loads[1:]:
+    for copy in loads:
         copy.wait()
     repack(0)
     forward(0, 0, 8)
@@ -229,25 +290,27 @@
     forward(0, 16, 8)
     relay(7)
     forward(0, 24, row_blocks - 24)
-    spread(0)
+    spread(0, 0, row_blocks)
+    collect(0)
     for c in range(4):
-        own[4 + c].wait_send()
         send_terms(c)
+    start_back(0)
     for c in range(4, FEATS):
         passed[c].wait_recv()
         across[c].wait_recv()
     repack(1)
     forward(1, 0, 16)
     hand_on(0)
+    back_sums[0].share()
     forward(1, 16, row_blocks - 16)
     hand_on(1)
-    act_out = pltpu.make_async_copy(actv, act_hbm, act_sem)
-    act_out.start()
-    for c in range(FEATS):
-        part[c] = jnp.dot(gp[c * slab : (c + 1) * slab, :], leftv[...], preferred_element_type=F32)
-    latent.drain()
-    back_sum = FeatSum(p, s, part, outgoing, landed2, shared2, (rs_send2, rs_recv2, ag_send2, ag_recv2))
-    back_sum.send()
+    act_outs = []
+    for h in range(2):
+        for c in range(FEATS):
+            act_outs.append(
+                pltpu.make_async_copy(part_of(actv, h, c), act_hbm.at[c, h], act_sem.at[h * FEATS + c])
+            )
+            act_outs[-1].start()
 
     def seq_at(half_, y_, core_):
         return half_ * 8 + y_ * 2 + core_
@@ -293,30 +356,48 @@
     cores[0].start()
     cores[1].start()
     hand_on(2)
-    hand_on(3)
-    spread(1)
-    for c in (4, 5, 6):
-        send_terms(c)
+    spread(1, 0, row_blocks // 2)
     for i in range(2):
         pair_sum(i)
         far[i].start()
-    back_sum.share()
+    hand_on(3)
+    spread(1, row_blocks // 2, row_blocks - row_blocks // 2)
+    collect(1)
+    for c in (4, 5, 6, 7):
+        send_terms(c)
     for h in (0, 1):
         grad_rows((1 - far_pair) * per_pair + h * 2 * per_pair, per_pair)
     for copy in cores[2:]:
         copy.start()
-    send_terms(7)
+    start_back(1)
+    end_back(0)
     pair_sum(3)
     near[1].start()
     pair_sum(4)
     near[2].start()
-    hand_on(4)
     pair_sum(2)
     pair_sum(5)
-    back_sum.finish()
-    for c in range(FEATS):
-        backv[c * slab : (c + 1) * slab, :] = shared2[c]
-    product = lax.dot_general(tokv[...], backv[...], (((0,), (0,)), ((), ())), preferred_element_type=F32) * norm_scale
+    hand_on(4)
+    finish_half(0)
+    back_sums[1].share()
+    far[0].wait_recv()
+    q[2] = (q[2].astype(F32) + ry2[0].astype(F32)).astype(BF16)
+    near[0].start()
+    far[1].wait_recv()
+    q[5] = (q[5].astype(F32) + ry2[1].astype(F32)).astype(BF16)
+    near[3].start()
+    hand_on(5)
+    hand_on(6)
+    pair_sum(6)
+    pair_sum(7)
+    hand_on(7)
+    end_back(1)
+    product = (
+        lax.dot_general(
+            tokv[...].reshape(rows, width), backv[...], (((0,), (0,)), ((), ())), preferred_element_type=F32
+        )
+        * norm_scale
+    )
     grow = gright.shape[0]
     for k in range(SEQS):
         grsend[k] = product[k * grow : (k + 1) * grow, :].astype(BF16)
@@ -326,35 +407,7 @@
     ]
     for copy in rights:
         copy.start()
-    hand_on(5)
-    far[0].wait_recv()
-    q[2] = (q[2].astype(F32) + ry2[0].astype(F32)).astype(BF16)
-    near[0].start()
-    far[1].wait_recv()
-    q[5] = (q[5].astype(F32) + ry2[1].astype(F32)).astype(BF16)
-    near[3].start()
-    hand_on(6)
-    hand_on(7)
-    pair_sum(6)
-    pair_sum(7)
-    for c in range(FEATS):
-        here = slice(c * slab, (c + 1) * slab)
-        low = lax.dot_general(backv[here, :], right[...], (((1,), (1,)), ((), ())), preferred_element_type=F32)
-        second[c].wait_recv()
-        upward[c].wait_recv()
-        terms[0, here, :] = (
-            low + terms[0, here, :].astype(F32) + rx2[here, :].astype(F32) + rz[here, :].astype(F32)
-        ).astype(BF16)
-    regroup = []
-    for k in range(1, FEATS):
-        there = (p + k) % FEATS
-        mine_rows = pl.ds(pl.multiple_of(there * slab, slab), slab)
-        regroup.append(
-            remote(terms.at[0, mine_rows, :], a2a.at[p], as_.at[k - 1], ar.at[k - 1], there, s)
-        )
-    for copy in regroup:
-        copy.start()
-    a2a[p] = terms[0, pl.ds(pl.multiple_of(p * slab, slab), slab), :]
+    finish_half(1)
     for copy in near:
         copy.wait_recv()
     zsend[...] = (q[6].astype(F32) + ry1[0].astype(F32) + ry1[2].astype(F32)).astype(BF16)
@@ -369,10 +422,13 @@
     grad[...] = q[7].astype(F32) + ry1[1].astype(F32) + ry1[3].astype(F32) + zrecv[...].astype(F32)
     for copy in regroup:
         copy.wait_recv()
-    back_sum.drain()
-    for copy in own[:4] + passed + across + first + second + upward + cores + far + near + rights + regroup + [cross]:
+    latent.drain()
+    for each in back_sums:
+        each.drain()
+    for copy in own + passed + across + first + second + upward + cores + far + near + rights + regroup + [cross]:
         copy.wait_send()
-    act_out.wait()
+    for copy in act_outs:
+        copy.wait()
 
 
 def chain_links(pattern, blocks):
@@ -398,15 +454,16 @@
     vmem_spec = pl.BlockSpec(memory_space=pltpu.VMEM)
     smem_spec = pl.BlockSpec(memory_space=pltpu.SMEM)
     dma = pltpu.SemaphoreType.DMA
-    d8, d7, d4, d2, d15 = dma((8,)), dma((7,)), dma((4,)), dma((2,)), dma((15,))
-    half = pltpu.VMEM((rows // 2, width), BF16)
+    d8, d7, d4, d2, d15, d27 = dma((8,)), dma((7,)), dma((4,)), dma((2,)), dma((15,)), dma((2, 7))
+    small = slab // 2
+    half = pltpu.VMEM((FEATS, small, width), BF16)
     whole = pltpu.VMEM((rows, width), BF16)
     slabs, slabs7 = pltpu.VMEM((FEATS, slab, rank), BF16), pltpu.VMEM((FEATS - 1, slab, rank), BF16)
     flat = pltpu.VMEM((rows, rank), BF16)
     return pl.pallas_call(
         functools.partial(kernel, norm_scale),
         out_shape=(
-            jax.ShapeDtypeStruct((rows, out_rows), BF16),
+            jax.ShapeDtypeStruct((FEATS, 2, slab // 2, out_rows), BF16),
             jax.ShapeDtypeStruct((FEATS, slab, width), BF16),
             jax.ShapeDtypeStruct((piece, all_wide), F32),
             jax.ShapeDtypeStruct((grow, rank), F32),
@@ -415,23 +472,32 @@
         out_specs=(any_spec, vmem_spec, vmem_spec, vmem_spec),
         scratch_shapes=[
             pltpu.VMEM((blocks, rows, wide), BF16),
-            whole, half, half, half, half, half, half,
+            pltpu.VMEM((2, FEATS, small, width), BF16), half, half, half, half, half, half,
             pltpu.VMEM((out_rows, wide), BF16), pltpu.VMEM((out_rows, rank), BF16),
             pltpu.VMEM((rows, out_rows), BF16), pltpu.VMEM((rows, out_rows), BF16),
             pltpu.VMEM((row_blocks + 1, rows // 2, wide), F32),
             pltpu.VMEM((LEVELS, rows, width), BF16),
             pltpu.VMEM((out_rows, all_wide), BF16),
-            pltpu.VMEM((FEATS, slab, rank), F32), slabs, slabs7, slabs, flat, slabs7, slabs, flat,
+            pltpu.VMEM((FEATS, slab, rank), F32), slabs, slabs7, slabs, flat,
+            pltpu.VMEM((2, FEATS, small, rank), F32), pltpu.VMEM((2, FEATS, small, rank), BF16),
+            pltpu.VMEM((2, FEATS - 1, small, rank), BF16), pltpu.VMEM((2, FEATS, small, rank), BF16), flat,
             whole, whole, whole,
             pltpu.VMEM((8, piece, all_wide), BF16), pltpu.VMEM((8, piece, all_wide), BF16),
             pltpu.VMEM((2, piece, all_wide), BF16), pltpu.VMEM((4, piece, all_wide), BF16),
             pltpu.VMEM((piece, all_wide), BF16), pltpu.VMEM((piece, all_wide), BF16),
             pltpu.VMEM((SEQS, grow, rank), BF16), pltpu.VMEM((SEQS - 1, grow, rank), BF16),
-            d4, d8, d8, d8, d8, d8, d8, d7, d7, d7, d7, d7, d7, d7, d7,
-            d8, d8, d8, d8, d8, d8, d7, d7, d8, d8, d2, d2, d4, d4, dma, dma, d15, d15, dma,
+            dma((20,)), d8, d8, d8, d8, d8, d8, d7, d7, d7, d7, d27, d27, d27, d27,
+            d8, d8, d8, d8, d8, d8, d27, d27, d8, d8, d2, d2, d4, d4, dma, dma, d15, d15, dma((16,)),
         ],
         compiler_params=pltpu.CompilerParams(collective_id=0, has_side_effects=True, vmem_limit_bytes=VMEM_LIMIT),
-    )(chain_links(pattern, blocks), tokens, weights, left, cotangent, right)
+    )(
+        chain_links(pattern, blocks),
+        tokens.reshape(FEATS, 2, slab // 2, width),
+        weights,
+        left,
+        cotangent.reshape(FEATS, 2, slab // 2, out_rows),
+        right,
+    )
 
 
 def place_kernel(wide, act, a2a, grad, gright, act_o, gin_o, gb_o, gl_o, gr_o, actv, a2av, gradv, grv, in_sem, out_sem):
@@ -481,7 +547,7 @@
             pltpu.VMEM(grad.shape, F32), pltpu.VMEM(gright.shape, F32),
             dma((14,)), dma((15,)),
         ],
-        compiler_params=pltpu.CompilerParams(vmem_limit_bytes=16 * 1024 * 1024),
+        compiler_params=pltpu.CompilerParams(vmem_limit_bytes=VMEM_LIMIT),
     )(act, a2a, grad, gright)
 
 
@@ -490,7 +556,9 @@
     act, a2a, grad, gright = fused(
         tokens, block_weights, left_factor, right_factor, pattern, cotangent, norm_scale
     )
-    activated, grad_input, grad_blocks, grad_left, grad_right = place(act, a2a, grad, gright, block_weights.shape[1])
+    activated, grad_input, grad_blocks, grad_left, grad_right = place(
+        act.reshape(cotangent.shape), a2a, grad, gright, block_weights.shape[1]
+    )
     return activated, grad_input[None], grad_blocks, grad_left, grad_right
 
 

time: 121 us -> 124 us (1.025)
  Pallas kernels: 112 us -> 120 us
  local copies, waits for them, and re-layouts: 5.2 us -> 0.01 us
    pallas_call x1, Pallas kernels: 107 us -> 116 us  [fused(): pl.pallas_call(functools.partial(kernel, norm_scale), out_shape=(jax.Shap...]
    unnamed x8 -> x0, local copies, waits for them, and re-layouts: 5.19 us -> none
where the time goes in v3:
time: 124 us; the launch traced here: 123 us
  Pallas kernels  120 us (97%)
  other arithmetic  2.1 us (2%)
    pallas_call x1, Pallas kernels, fused(): pl.pallas_call(functools.partial(kernel, norm_scale), out_shape=(jax.Shap...  116 us
    pallas_call x1, Pallas kernels, place(): pl.pallas_call(functools.partial(place_kernel, wide), out_shape=(jax.Shap...  4.53 us

profile of v3, /device:TPU:0, one launch (start us, length us, event | category | flops | bytes accessed | tf_op | source)
XLA Modules:
  0.0 123.1 jit_solution(2512048001048029516)
XLA Ops:
  0.6 0.7 and_select_fusion
  1.3 0.1 pad_add_fusion
  1.4 0.7 select_reduce_fusion
  2.2 0.6 pad_add_fusion.1.refs_0_
  2.7 115.6 %shard_map.101 = (bf16[8,2,32,3584]{3,2,1,0:T(8,128)(2,1)}, bf16[8,64,1024]{2,1,0:T(8,128)(2,1)}, f32[224,768]{1,0:T(8,128)}, f32[64,256]{1,0:T(8,128)}) custom-call(s32[64]{0:T(128)} %pad_add_fusion.1.refs_0_, bf16[8,2,32,1024]{3,2,1,0:T(8,128)(2,1)} %bitcast.8, bf16[3584,512]{1,0:T(8,128)(2,1)} %refs_2_.1, bf16[3584,256]{1,0:T(8,128)(2,1)} %refs_3_.1, ...), custom_call_target="tpu_custom_call" | custom-call | tf_op jit(solution)/shard_map/pallas_call | solution.py:463
  118.4 4.5 %shard_map.102 = (bf16[512,3584]{1,0:T(8,128)(2,1)}, bf16[64,8192]{1,0:T(8,128)(2,1)}, f32[224,512]{1,0:T(8,128)}, f32[224,256]{1,0:T(8,128)}, f32[64,256]{1,0:T(8,128)}) custom-call(bf16[512,3584]{1,0:T(8,128)(2,1)} %bitcast.6, bf16[8,64,1024]{2,1,0:T(8,128)(2,1)} %get-tuple-element.15.a2a, f32[224,768]{1,0:T(8,128)} %get-tuple-element.16.grad, ...), custom_call_target="tpu_custom_call" | custom-call | tf_op jit(solution)/shard_map/pallas_call | solution.py:534
  (2 shorter events, 0.0 us)

commit v4 on v3

--- a/solution.py
+++ b/solution.py
@@ -94,13 +94,13 @@
     (
         xall, tokv, x1a, x1b, x2a, x2b, x3a, x3b, wv, leftv, gp, actv, sums, terms, grads,
         part, outgoing, landed, shared, lat, backp, backo, backl, backs, backv, rx1, rx2, rz,
-        crecv, q, ry2, ry1, zsend, zrecv, grsend, grrecv,
-    ) = refs[10:46]
+        crecv, q, ry2, ry1, zsend, zrecv, grsend, grpair, grsum, grrecv,
+    ) = refs[10:48]
     (
         lsem, x_send, x_recv, f_send, f_recv, z_send, z_recv, rs_send, rs_recv, ag_send, ag_recv,
         rs_send2, rs_recv2, ag_send2, ag_recv2, x1s, x1r, x2s, x2r, zs, zr, as_, ar,
-        cs, cr, y2s, y2r, y1s, y1r, hs, hr, gs, gr, act_sem,
-    ) = refs[46:]
+        cs, cr, y2s, y2r, y1s, y1r, hs, hr, gps, gpr, gs, gr, act_sem,
+    ) = refs[48:]
     p, s = lax.axis_index("feat"), lax.axis_index("seq")
     x, z = p // 2, p % 2
     side, back, up = 2 * (x + 1 - 2 * (x % 2)) + z, 2 * (3 - x) + z, 2 * x + 1 - z
@@ -112,7 +112,7 @@
     blocks = width // BLK
     row_blocks = wv.shape[0] // BLK
     wide = LEVELS * BLK
-    piece = q.shape[1]
+    piece = crecv.shape[1]
 
     def part_of(ref, h, c):
         return ref.at[pl.ds(h * mid_rows + c * small, small), :]
@@ -155,7 +155,7 @@
         own[c].start()
         across[c].start()
 
-    sums[row_blocks] = jnp.zeros(sums.shape[1:], F32)
+    sums[0] = jnp.zeros(sums.shape[1:], F32)
 
     def relay(c):
         own[c].wait_recv()
@@ -204,7 +204,7 @@
 
         def one(f):
             fr = block_of(f)
-            sums[f] = sums[links[f]] + jnp.dot(gp[here, fr], wv[fr, :], preferred_element_type=F32)
+            sums[f + 1] = sums[links[f]] + jnp.dot(gp[here, fr], wv[fr, :], preferred_element_type=F32)
 
         loop(begin, count, one)
 
@@ -260,9 +260,12 @@
             regroup.append(remote(src, dst, as_.at[h, k - 1], ar.at[h, k - 1], there, s))
 
     def finish_half(h):
+        lows = lax.dot_general(
+            backv[halves(h), :], right[...], (((1,), (1,)), ((), ())), preferred_element_type=F32
+        )
         for c in range(h * 4, h * 4 + 4):
             here = slice(c * slab, (c + 1) * slab)
-            low = lax.dot_general(backv[here, :], right[...], (((1,), (1,)), ((), ())), preferred_element_type=F32)
+            low = lows[(c % 4) * slab : (c % 4 + 1) * slab, :]
             second[c].wait_recv()
             upward[c].wait_recv()
             terms[0, here, :] = (
@@ -283,27 +286,28 @@
     for copy in loads:
         copy.wait()
     repack(0)
-    forward(0, 0, 8)
+    forward(0, 0, 12)
     relay(5)
-    forward(0, 8, 8)
+    forward(0, 12, row_blocks - 12)
     relay(6)
-    forward(0, 16, 8)
+    spread(0, 0, row_blocks // 2)
     relay(7)
-    forward(0, 24, row_blocks - 24)
-    spread(0, 0, row_blocks)
+    spread(0, row_blocks // 2, row_blocks - row_blocks // 2)
     collect(0)
-    for c in range(4):
-        send_terms(c)
     start_back(0)
+    send_terms(0)
+    send_terms(1)
     for c in range(4, FEATS):
         passed[c].wait_recv()
         across[c].wait_recv()
     repack(1)
-    forward(1, 0, 16)
+    forward(1, 0, 12)
     hand_on(0)
+    send_terms(2)
     back_sums[0].share()
-    forward(1, 16, row_blocks - 16)
+    forward(1, 12, row_blocks - 12)
     hand_on(1)
+    send_terms(3)
     act_outs = []
     for h in range(2):
         for c in range(FEATS):
@@ -344,53 +348,51 @@
     ]
     near = [remote(q.at[2 + i], ry1.at[i], y1s.at[i], y1r.at[i], p, up_y if i < 2 else down_y) for i in range(4)]
 
-    def pair_sum(i):
+    def pair_sum(i, *others):
         dy, h = slots[i]
+        total = grads[rows_of(dy, h, core), :].astype(F32) + crecv[i].astype(F32)
+        for other in others:
+            total = total + other[...].astype(F32)
+        return total
+
+    def send_sum(i, copy, *others):
         cores[i].wait_recv()
-        q[i] = (grads[rows_of(dy, h, core), :].astype(F32) + crecv[i].astype(F32)).astype(BF16)
+        q[i] = pair_sum(i, *others).astype(BF16)
+        copy.start()
 
     far_pair = ((y + 2) % 4) // 2
     per_pair = row_blocks // 4
+    spread(1, 0, row_blocks)
+    collect(1)
+    hand_on(2)
+    send_terms(4)
+    send_terms(5)
+    start_back(1)
     for h in (0, 1):
         grad_rows(far_pair * per_pair + h * 2 * per_pair, per_pair)
     cores[0].start()
     cores[1].start()
-    hand_on(2)
-    spread(1, 0, row_blocks // 2)
-    for i in range(2):
-        pair_sum(i)
-        far[i].start()
     hand_on(3)
-    spread(1, row_blocks // 2, row_blocks - row_blocks // 2)
-    collect(1)
-    for c in (4, 5, 6, 7):
-        send_terms(c)
     for h in (0, 1):
         grad_rows((1 - far_pair) * per_pair + h * 2 * per_pair, per_pair)
-    for copy in cores[2:]:
-        copy.start()
-    start_back(1)
+    for i in (4, 2, 3, 5, 6, 7):
+        cores[i].start()
+    for i in range(2):
+        send_sum(i, far[i])
     end_back(0)
-    pair_sum(3)
-    near[1].start()
-    pair_sum(4)
-    near[2].start()
-    pair_sum(2)
-    pair_sum(5)
+    finish_half(0)
+    send_sum(4, near[2])
     hand_on(4)
-    finish_half(0)
+    send_terms(6)
     back_sums[1].share()
+    hand_on(5)
+    send_terms(7)
     far[0].wait_recv()
-    q[2] = (q[2].astype(F32) + ry2[0].astype(F32)).astype(BF16)
-    near[0].start()
+    send_sum(2, near[0], ry2.at[0])
+    send_sum(3, near[1])
     far[1].wait_recv()
-    q[5] = (q[5].astype(F32) + ry2[1].astype(F32)).astype(BF16)
-    near[3].start()
-    hand_on(5)
+    send_sum(5, near[3], ry2.at[1])
     hand_on(6)
-    pair_sum(6)
-    pair_sum(7)
-    hand_on(7)
     end_back(1)
     product = (
         lax.dot_general(
@@ -400,32 +402,42 @@
     )
     grow = gright.shape[0]
     for k in range(SEQS):
-        grsend[k] = product[k * grow : (k + 1) * grow, :].astype(BF16)
-    rights = [
-        remote(grsend.at[(s + k) % SEQS], grrecv.at[k - 1], gs.at[k - 1], gr.at[k - 1], p, (s + k) % SEQS)
-        for k in range(1, SEQS)
-    ]
+        grsend[k // 2, k % 2] = product[k * grow : (k + 1) * grow, :].astype(BF16)
+    pair = remote(grsend.at[:, 1 - core], grpair, gps, gpr, p, sibling)
+    pair.start()
+    place_ = half * 4 + y
+    rights = []
+    for k in range(1, SEQS // 2):
+        there = (place_ + k) % (SEQS // 2)
+        rights.append(
+            remote(grsum.at[there], grrecv.at[k - 1], gs.at[k - 1], gr.at[k - 1], p, there * 2 + core)
+        )
+    hand_on(7)
+    pair.wait_recv()
+    grsum[...] = (grsend[:, core].astype(F32) + grpair[...].astype(F32)).astype(BF16)
     for copy in rights:
         copy.start()
     finish_half(1)
-    for copy in near:
+    for copy in (near[0], near[2], cores[6]):
         copy.wait_recv()
-    zsend[...] = (q[6].astype(F32) + ry1[0].astype(F32) + ry1[2].astype(F32)).astype(BF16)
+    zsend[...] = pair_sum(6, ry1.at[0], ry1.at[2]).astype(BF16)
     cross = remote(zsend, zrecv, hs, hr, p, other_half)
     cross.start()
-    total = grsend[s].astype(F32)
+    for copy in (near[1], near[3], cores[7]):
+        copy.wait_recv()
+    total = grsend[place_, core].astype(F32) + grpair[place_].astype(F32)
     for k, copy in enumerate(rights):
         copy.wait_recv()
         total = total + grrecv[k].astype(F32)
     gright[...] = total
     cross.wait_recv()
-    grad[...] = q[7].astype(F32) + ry1[1].astype(F32) + ry1[3].astype(F32) + zrecv[...].astype(F32)
+    grad[...] = pair_sum(7, ry1.at[1], ry1.at[3], zrecv)
     for copy in regroup:
         copy.wait_recv()
     latent.drain()
     for each in back_sums:
         each.drain()
-    for copy in own + passed + across + first + second + upward + cores + far + near + rights + regroup + [cross]:
+    for copy in own + passed + across + first + second + upward + cores + far + near + rights + regroup + [cross, pair]:
         copy.wait_send()
     for copy in act_outs:
         copy.wait()
@@ -433,13 +445,17 @@
 
 def chain_links(pattern, blocks):
     count = pattern.shape[0]
-    places = pattern[:, 0] % blocks
-    rows = jnp.arange(count)
-    wanted = jnp.concatenate([places, jnp.arange(blocks, dtype=places.dtype)])
-    limit = jnp.concatenate([rows, jnp.full((blocks,), count)])
-    found = (wanted[:, None] == places[None, :]) & (rows[None, :] < limit[:, None])
-    latest = jnp.max(jnp.where(found, rows[None, :], -1), axis=1)
-    return jnp.concatenate([jnp.where(latest < 0, count, latest), places]).astype(jnp.int32)
+    total = 2 * count + blocks
+    place = lax.rem(pattern[:, 0], blocks)
+    r = lax.broadcasted_iota(jnp.int32, (total, count), 0)
+    g = lax.broadcasted_iota(jnp.int32, (total, count), 1)
+    across = jnp.broadcast_to(place[None, :], (total, count))
+    down = jnp.broadcast_to(jnp.pad(place, (0, total - count))[:, None], (total, count))
+    is_row, is_place = r < count, r < count + blocks
+    linked = jnp.where(is_row, (down == across) & (g < r), across == r - count)
+    found = jnp.where(linked, g + 1, 0)
+    own = jnp.where(g == r - count - blocks, across, 0)
+    return jnp.max(jnp.where(is_place, found, own), axis=1)
 
 
 def fused(tokens, weights, left, right, pattern, cotangent, norm_scale):
@@ -454,7 +470,7 @@
     vmem_spec = pl.BlockSpec(memory_space=pltpu.VMEM)
     smem_spec = pl.BlockSpec(memory_space=pltpu.SMEM)
     dma = pltpu.SemaphoreType.DMA
-    d8, d7, d4, d2, d15, d27 = dma((8,)), dma((7,)), dma((4,)), dma((2,)), dma((15,)), dma((2, 7))
+    d8, d7, d4, d2, d27 = dma((8,)), dma((7,)), dma((4,)), dma((2,)), dma((2, 7))
     small = slab // 2
     half = pltpu.VMEM((FEATS, small, width), BF16)
     whole = pltpu.VMEM((rows, width), BF16)
@@ -482,12 +498,13 @@
             pltpu.VMEM((2, FEATS, small, rank), F32), pltpu.VMEM((2, FEATS, small, rank), BF16),
             pltpu.VMEM((2, FEATS - 1, small, rank), BF16), pltpu.VMEM((2, FEATS, small, rank), BF16), flat,
             whole, whole, whole,
-            pltpu.VMEM((8, piece, all_wide), BF16), pltpu.VMEM((8, piece, all_wide), BF16),
+            pltpu.VMEM((8, piece, all_wide), BF16), pltpu.VMEM((6, piece, all_wide), BF16),
             pltpu.VMEM((2, piece, all_wide), BF16), pltpu.VMEM((4, piece, all_wide), BF16),
             pltpu.VMEM((piece, all_wide), BF16), pltpu.VMEM((piece, all_wide), BF16),
-            pltpu.VMEM((SEQS, grow, rank), BF16), pltpu.VMEM((SEQS - 1, grow, rank), BF16),
+            pltpu.VMEM((SEQS // 2, 2, grow, rank), BF16), pltpu.VMEM((SEQS // 2, grow, rank), BF16),
+            pltpu.VMEM((SEQS // 2, grow, rank), BF16), pltpu.VMEM((SEQS // 2 - 1, grow, rank), BF16),
             dma((20,)), d8, d8, d8, d8, d8, d8, d7, d7, d7, d7, d27, d27, d27, d27,
-            d8, d8, d8, d8, d8, d8, d27, d27, d8, d8, d2, d2, d4, d4, dma, dma, d15, d15, dma((16,)),
+            d8, d8, d8, d8, d8, d8, d27, d27, d8, d8, d2, d2, d4, d4, dma, dma, dma, dma, d7, d7, dma((16,)),
         ],
         compiler_params=pltpu.CompilerParams(collective_id=0, has_side_effects=True, vmem_limit_bytes=VMEM_LIMIT),
     )(

time: 124 us -> 111 us (0.90)
  Pallas kernels: 120 us -> 108 us
    pallas_call x1, Pallas kernels: 116 us -> 104 us  [fused(): pl.pallas_call(functools.partial(kernel, norm_scale), out_shape=(jax.Shap...]
where the time goes in v4:
time: 111 us; the launch traced here: 110 us
  Pallas kernels  108 us (97%)
  other arithmetic  1.3 us (1%)
    pallas_call x1, Pallas kernels, fused(): pl.pallas_call(functools.partial(kernel, norm_scale), out_shape=(jax.Shap...  104 us
    pallas_call x1, Pallas kernels, place(): pl.pallas_call(functools.partial(place_kernel, wide), out_shape=(jax.Shap...  4.53 us

profile of v4, /device:TPU:0, one launch (start us, length us, event | category | flops | bytes accessed | tf_op | source)
XLA Modules:
  0.0 110.4 jit_solution(15336103178558702862)
XLA Ops:
  0.6 0.7 compare_select_fusion
  1.3 0.6 select_reduce_fusion.refs_0_
  1.9 103.8 %shard_map.101 = (bf16[8,2,32,3584]{3,2,1,0:T(8,128)(2,1)}, bf16[8,64,1024]{2,1,0:T(8,128)(2,1)}, f32[224,768]{1,0:T(8,128)}, f32[64,256]{1,0:T(8,128)}) custom-call(s32[64]{0:T(128)} %select_reduce_fusion.refs_0_, bf16[8,2,32,1024]{3,2,1,0:T(8,128)(2,1)} %bitcast.8, bf16[3584,512]{1,0:T(8,128)(2,1)} %refs_2_.1, bf16[3584,256]{1,0:T(8,128)(2,1)} %refs_3_.1, ...), custom_call_target="tpu_custom_call" | custom-call | tf_op jit(solution)/shard_map/pallas_call | solution.py:479
  105.7 4.5 %shard_map.102 = (bf16[512,3584]{1,0:T(8,128)(2,1)}, bf16[64,8192]{1,0:T(8,128)(2,1)}, f32[224,512]{1,0:T(8,128)}, f32[224,256]{1,0:T(8,128)}, f32[64,256]{1,0:T(8,128)}) custom-call(bf16[512,3584]{1,0:T(8,128)(2,1)} %bitcast.6, bf16[8,64,1024]{2,1,0:T(8,128)(2,1)} %get-tuple-element.15.a2a, f32[224,768]{1,0:T(8,128)} %get-tuple-element.16.grad, ...), custom_call_target="tpu_custom_call" | custom-call | tf_op jit(solution)/shard_map/pallas_call | solution.py:551
  (3 shorter events, 0.0 us)

commit v5 on v4

--- a/solution.py
+++ b/solution.py
@@ -3,6 +3,7 @@
 
 import jax
 import jax.numpy as jnp
+import numpy as np
 from jax import lax
 from jax.experimental import pallas as pl
 from jax.experimental.pallas import tpu as pltpu
@@ -34,7 +35,7 @@
     barrier = pltpu.get_barrier_semaphore()
     for feat, seq in devices:
         pl.semaphore_signal(barrier, inc=1, device_id=(feat, seq), device_id_type=MESH)
-    pl.semaphore_wait(barrier, len(devices))
+    return lambda: pl.semaphore_wait(barrier, len(devices))
 
 
 class FeatSum:
@@ -49,8 +50,10 @@
             )
             self.ag.append(remote(shared.at[p], shared.at[p], ag_send.at[k - 1], ag_recv.at[k - 1], there, s))
 
+    def cast(self):
+        self.outgoing[...] = self.part[...].astype(BF16)
+
     def send(self):
-        self.outgoing[...] = self.part[...].astype(BF16)
         for copy in self.rs:
             copy.start()
 
@@ -126,7 +129,7 @@
             )
     for copy in tok_loads + loads:
         copy.start()
-    greet([((p + k) % FEATS, s) for k in range(1, FEATS)] + [(p, (s + k) % SEQS) for k in range(1, SEQS)])
+    all_here = greet([((p + k) % FEATS, s) for k in range(1, FEATS)] + [(p, (s + k) % SEQS) for k in range(1, SEQS)])
 
     def chunk(pair, c):
         return pair[c // 4].at[pl.ds((c % 4) * 2, 2)]
@@ -143,31 +146,40 @@
     ]
     across = [remote(own_chunk(c), chunk((x3a, x3b), c), z_send.at[c], z_recv.at[c], up, s) for c in range(FEATS)]
     latent = FeatSum(p, s, part, outgoing, landed, shared, (rs_send, rs_recv, ag_send, ag_recv))
-    own[0].start()
-    across[0].start()
     for copy in tok_loads:
         copy.wait()
     for c in range(FEATS):
         mine = tokv[c // 4, (c % 4) * 2 : (c % 4) * 2 + 2].reshape(slab, width)
         part[c] = jnp.dot(mine, right[...], preferred_element_type=F32)
+    latent.cast()
+    all_here()
     latent.send()
-    for c in (1,):
+
+    def send_own(c):
         own[c].start()
         across[c].start()
+
+    send_own(0)
 
     sums[0] = jnp.zeros(sums.shape[1:], F32)
 
     def relay(c):
         own[c].wait_recv()
         passed[c].start()
-        if c + 2 < FEATS:
-            own[c + 2].start()
-            across[c + 2].start()
-
+
+    latent.share()
+    send_own(1)
+    send_own(2)
     relay(0)
-    latent.share()
-    for c in range(1, 5):
-        relay(c)
+    send_own(3)
+    relay(1)
+    send_own(4)
+    relay(2)
+    send_own(5)
+    send_own(6)
+    relay(3)
+    send_own(7)
+    relay(4)
 
     def halves(h):
         return slice(h * mid_rows, (h + 1) * mid_rows)
@@ -244,6 +256,7 @@
                 wider = slice(h * mid_rows + c * small, h * mid_rows + (c + 4) * small)
                 four = jnp.dot(gp[wider, :], leftv[...], preferred_element_type=F32)
             backp[h, c] = four[(c % 4) * small : (c % 4 + 1) * small, :]
+        back_sums[h].cast()
         back_sums[h].send()
 
     def end_back(h):
@@ -362,36 +375,37 @@
 
     far_pair = ((y + 2) % 4) // 2
     per_pair = row_blocks // 4
-    spread(1, 0, row_blocks)
-    collect(1)
-    hand_on(2)
-    send_terms(4)
-    send_terms(5)
-    start_back(1)
     for h in (0, 1):
         grad_rows(far_pair * per_pair + h * 2 * per_pair, per_pair)
     cores[0].start()
     cores[1].start()
+    spread(1, 0, row_blocks // 2)
+    for i in range(2):
+        send_sum(i, far[i])
+    hand_on(2)
+    spread(1, row_blocks // 2, row_blocks - row_blocks // 2)
+    collect(1)
+    start_back(1)
+    send_terms(4)
+    send_terms(5)
     hand_on(3)
+    send_terms(6)
     for h in (0, 1):
         grad_rows((1 - far_pair) * per_pair + h * 2 * per_pair, per_pair)
     for i in (4, 2, 3, 5, 6, 7):
         cores[i].start()
-    for i in range(2):
-        send_sum(i, far[i])
+    hand_on(4)
+    send_terms(7)
     end_back(0)
     finish_half(0)
     send_sum(4, near[2])
-    hand_on(4)
-    send_terms(6)
-    back_sums[1].share()
-    hand_on(5)
-    send_terms(7)
     far[0].wait_recv()
     send_sum(2, near[0], ry2.at[0])
     send_sum(3, near[1])
     far[1].wait_recv()
     send_sum(5, near[3], ry2.at[1])
+    hand_on(5)
+    back_sums[1].share()
     hand_on(6)
     end_back(1)
     product = (
@@ -417,12 +431,12 @@
     grsum[...] = (grsend[:, core].astype(F32) + grpair[...].astype(F32)).astype(BF16)
     for copy in rights:
         copy.start()
-    finish_half(1)
     for copy in (near[0], near[2], cores[6]):
         copy.wait_recv()
     zsend[...] = pair_sum(6, ry1.at[0], ry1.at[2]).astype(BF16)
     cross = remote(zsend, zrecv, hs, hr, p, other_half)
     cross.start()
+    finish_half(1)
     for copy in (near[1], near[3], cores[7]):
         copy.wait_recv()
     total = grsend[place_, core].astype(F32) + grpair[place_].astype(F32)
@@ -447,15 +461,13 @@
     count = pattern.shape[0]
     total = 2 * count + blocks
     place = lax.rem(pattern[:, 0], blocks)
-    r = lax.broadcasted_iota(jnp.int32, (total, count), 0)
-    g = lax.broadcasted_iota(jnp.int32, (total, count), 1)
+    r, g = np.arange(total)[:, None], np.arange(count)[None, :]
     across = jnp.broadcast_to(place[None, :], (total, count))
     down = jnp.broadcast_to(jnp.pad(place, (0, total - count))[:, None], (total, count))
-    is_row, is_place = r < count, r < count + blocks
-    linked = jnp.where(is_row, (down == across) & (g < r), across == r - count)
-    found = jnp.where(linked, g + 1, 0)
+    linked = jnp.where(r < count, (down == across) & (g < r), across == np.broadcast_to(r - count, (total, count)))
+    found = jnp.where(linked, np.int32(g + 1), 0)
     own = jnp.where(g == r - count - blocks, across, 0)
-    return jnp.max(jnp.where(is_place, found, own), axis=1)
+    return jnp.max(jnp.where(r < count + blocks, found, own), axis=1).astype(jnp.int32)
 
 
 def fused(tokens, weights, left, right, pattern, cotangent, norm_scale):

time: 111 us -> 117 us (1.054)
  Pallas kernels: 108 us -> 113 us
    pallas_call x1, Pallas kernels: 104 us -> 109 us  [fused(): pl.pallas_call(functools.partial(kernel, norm_scale), out_shape=(jax.Shap...]
where the time goes in v5:
time: 117 us; the launch traced here: 116 us
  Pallas kernels  113 us (97%)
  other arithmetic  2.03 us (2%)
    pallas_call x1, Pallas kernels, fused(): pl.pallas_call(functools.partial(kernel, norm_scale), out_shape=(jax.Shap...  109 us
    pallas_call x1, Pallas kernels, place(): pl.pallas_call(functools.partial(place_kernel, wide), out_shape=(jax.Shap...  4.53 us

profile of v5, /device:TPU:0, one launch (start us, length us, event | category | flops | bytes accessed | tf_op | source)
XLA Modules:
  0.0 116.0 jit_solution(16800655475799316598)
XLA Ops:
  0.6 0.7 compare_select_fusion
  1.3 1.3 %select_reduce_fusion.refs_0_ = s32[64]{0:T(128)} fusion(pred[64,28]{0,1:T(8,128)(4,1)} %constant.24.clone, s32[64,28]{0,1:T(8,128)} %constant.21.clone, pred[64,28]{0,1:T(8,128)(4,1)} %constant.20.clone, s32[28]{0:T(128)} %constant.31, s32[64]{0:T(128)S(1)} %pad.4, s32[28]{0:T(128)S(1)} %compare_select_fusion, pred[64]{0:T(512)(128)(4,1)} %constant.30, ...), kind=kLoop, calls=%fused_computation | loop fusion | flops 14272 | bytes 11616 | tf_op jit(solution)/shard_map/reduce_max | solution.py:470
  2.7 108.7 %shard_map.155 = (bf16[8,2,32,3584]{3,2,1,0:T(8,128)(2,1)}, bf16[8,64,1024]{2,1,0:T(8,128)(2,1)}, f32[224,768]{1,0:T(8,128)}, f32[64,256]{1,0:T(8,128)}) custom-call(s32[64]{0:T(128)} %select_reduce_fusion.refs_0_, bf16[8,2,32,1024]{3,2,1,0:T(8,128)(2,1)} %bitcast.8, bf16[3584,512]{1,0:T(8,128)(2,1)} %refs_2_.1, bf16[3584,256]{1,0:T(8,128)(2,1)} %refs_3_.1, ...), custom_call_target="tpu_custom_call" | custom-call | tf_op jit(solution)/shard_map/pallas_call | solution.py:491
  111.3 4.5 %shard_map.156 = (bf16[512,3584]{1,0:T(8,128)(2,1)}, bf16[64,8192]{1,0:T(8,128)(2,1)}, f32[224,512]{1,0:T(8,128)}, f32[224,256]{1,0:T(8,128)}, f32[64,256]{1,0:T(8,128)}) custom-call(bf16[512,3584]{1,0:T(8,128)(2,1)} %bitcast.6, bf16[8,64,1024]{2,1,0:T(8,128)(2,1)} %get-tuple-element.15.a2a, f32[224,768]{1,0:T(8,128)} %get-tuple-element.16.grad, ...), custom_call_target="tpu_custom_call" | custom-call | tf_op jit(solution)/shard_map/pallas_call | solution.py:563
  (1 shorter events, 0.0 us)

commit v6 on v4

--- a/solution.py
+++ b/solution.py
@@ -3,6 +3,7 @@
 
 import jax
 import jax.numpy as jnp
+import numpy as np
 from jax import lax
 from jax.experimental import pallas as pl
 from jax.experimental.pallas import tpu as pltpu
@@ -362,37 +363,37 @@
 
     far_pair = ((y + 2) % 4) // 2
     per_pair = row_blocks // 4
-    spread(1, 0, row_blocks)
-    collect(1)
-    hand_on(2)
-    send_terms(4)
-    send_terms(5)
-    start_back(1)
     for h in (0, 1):
         grad_rows(far_pair * per_pair + h * 2 * per_pair, per_pair)
     cores[0].start()
     cores[1].start()
+    spread(1, 0, row_blocks // 2)
+    for i in range(2):
+        send_sum(i, far[i])
+    hand_on(2)
+    spread(1, row_blocks // 2, row_blocks - row_blocks // 2)
+    collect(1)
     hand_on(3)
+    start_back(1)
+    send_terms(4)
+    send_terms(5)
     for h in (0, 1):
         grad_rows((1 - far_pair) * per_pair + h * 2 * per_pair, per_pair)
     for i in (4, 2, 3, 5, 6, 7):
         cores[i].start()
-    for i in range(2):
-        send_sum(i, far[i])
-    end_back(0)
-    finish_half(0)
+    back_sums[1].share()
     send_sum(4, near[2])
     hand_on(4)
     send_terms(6)
-    back_sums[1].share()
-    hand_on(5)
-    send_terms(7)
     far[0].wait_recv()
     send_sum(2, near[0], ry2.at[0])
     send_sum(3, near[1])
     far[1].wait_recv()
     send_sum(5, near[3], ry2.at[1])
-    hand_on(6)
+    hand_on(5)
+    send_terms(7)
+    end_back(0)
+    finish_half(0)
     end_back(1)
     product = (
         lax.dot_general(
@@ -412,17 +413,18 @@
         rights.append(
             remote(grsum.at[there], grrecv.at[k - 1], gs.at[k - 1], gr.at[k - 1], p, there * 2 + core)
         )
-    hand_on(7)
+    hand_on(6)
     pair.wait_recv()
     grsum[...] = (grsend[:, core].astype(F32) + grpair[...].astype(F32)).astype(BF16)
     for copy in rights:
         copy.start()
-    finish_half(1)
     for copy in (near[0], near[2], cores[6]):
         copy.wait_recv()
     zsend[...] = pair_sum(6, ry1.at[0], ry1.at[2]).astype(BF16)
     cross = remote(zsend, zrecv, hs, hr, p, other_half)
     cross.start()
+    hand_on(7)
+    finish_half(1)
     for copy in (near[1], near[3], cores[7]):
         copy.wait_recv()
     total = grsend[place_, core].astype(F32) + grpair[place_].astype(F32)
@@ -447,15 +449,13 @@
     count = pattern.shape[0]
     total = 2 * count + blocks
     place = lax.rem(pattern[:, 0], blocks)
-    r = lax.broadcasted_iota(jnp.int32, (total, count), 0)
-    g = lax.broadcasted_iota(jnp.int32, (total, count), 1)
+    r, g = np.arange(total)[:, None], np.arange(count)[None, :]
     across = jnp.broadcast_to(place[None, :], (total, count))
     down = jnp.broadcast_to(jnp.pad(place, (0, total - count))[:, None], (total, count))
-    is_row, is_place = r < count, r < count + blocks
-    linked = jnp.where(is_row, (down == across) & (g < r), across == r - count)
-    found = jnp.where(linked, g + 1, 0)
+    linked = jnp.where(r < count, (down == across) & (g < r), across == np.broadcast_to(r - count, (total, count)))
+    found = jnp.where(linked, np.int32(g + 1), 0)
     own = jnp.where(g == r - count - blocks, across, 0)
-    return jnp.max(jnp.where(is_place, found, own), axis=1)
+    return jnp.max(jnp.where(r < count + blocks, found, own), axis=1).astype(jnp.int32)
 
 
 def fused(tokens, weights, left, right, pattern, cotangent, norm_scale):

time: 111 us -> 111 us (level)
  no operation moved by 1% of the time
where the time goes in v6:
time: 111 us; the launch traced here: 110 us
  Pallas kernels  108 us (97%)
  other arithmetic  2.03 us (2%)
    pallas_call x1, Pallas kernels, fused(): pl.pallas_call(functools.partial(kernel, norm_scale), out_shape=(jax.Shap...  103 us
    pallas_call x1, Pallas kernels, place(): pl.pallas_call(functools.partial(place_kernel, wide), out_shape=(jax.Shap...  4.53 us

profile of v6, /device:TPU:0, one launch (start us, length us, event | category | flops | bytes accessed | tf_op | source)
XLA Modules:
  0.0 110.4 jit_solution(3394102885471666569)
XLA Ops:
  0.6 0.7 compare_select_fusion
  1.3 1.3 %select_reduce_fusion.refs_0_ = s32[64]{0:T(128)} fusion(pred[64,28]{0,1:T(8,128)(4,1)} %constant.24.clone, s32[64,28]{0,1:T(8,128)} %constant.21.clone, pred[64,28]{0,1:T(8,128)(4,1)} %constant.20.clone, s32[28]{0:T(128)} %constant.31, s32[64]{0:T(128)S(1)} %pad.4, s32[28]{0:T(128)S(1)} %compare_select_fusion, pred[64]{0:T(512)(128)(4,1)} %constant.30, ...), kind=kLoop, calls=%fused_computation | loop fusion | flops 14272 | bytes 11616 | tf_op jit(solution)/shard_map/reduce_max | solution.py:458
  2.7 103.0 %shard_map.155 = (bf16[8,2,32,3584]{3,2,1,0:T(8,128)(2,1)}, bf16[8,64,1024]{2,1,0:T(8,128)(2,1)}, f32[224,768]{1,0:T(8,128)}, f32[64,256]{1,0:T(8,128)}) custom-call(s32[64]{0:T(128)} %select_reduce_fusion.refs_0_, bf16[8,2,32,1024]{3,2,1,0:T(8,128)(2,1)} %bitcast.8, bf16[3584,512]{1,0:T(8,128)(2,1)} %refs_2_.1, bf16[3584,256]{1,0:T(8,128)(2,1)} %refs_3_.1, ...), custom_call_target="tpu_custom_call" | custom-call | tf_op jit(solution)/shard_map/pallas_call | solution.py:479
  105.7 4.5 %shard_map.156 = (bf16[512,3584]{1,0:T(8,128)(2,1)}, bf16[64,8192]{1,0:T(8,128)(2,1)}, f32[224,512]{1,0:T(8,128)}, f32[224,256]{1,0:T(8,128)}, f32[64,256]{1,0:T(8,128)}) custom-call(bf16[512,3584]{1,0:T(8,128)(2,1)} %bitcast.6, bf16[8,64,1024]{2,1,0:T(8,128)(2,1)} %get-tuple-element.15.a2a, f32[224,768]{1,0:T(8,128)} %get-tuple-element.16.grad, ...), custom_call_target="tpu_custom_call" | custom-call | tf_op jit(solution)/shard_map/pallas_call | solution.py:551
  (1 shorter events, 0.0 us)

commit v7 on v4

--- a/solution.py
+++ b/solution.py
@@ -518,7 +518,7 @@
 
 
 def place_kernel(wide, act, a2a, grad, gright, act_o, gin_o, gb_o, gl_o, gr_o, actv, a2av, gradv, grv, in_sem, out_sem):
-    parts = 4
+    parts = 8
     step = act.shape[0] // parts
     width = a2a.shape[2]
     rows = [pl.ds(i * step, step) for i in range(parts)]
@@ -562,7 +562,7 @@
         scratch_shapes=[
             pltpu.VMEM(act.shape, BF16), pltpu.VMEM(a2a.shape, BF16),
             pltpu.VMEM(grad.shape, F32), pltpu.VMEM(gright.shape, F32),
-            dma((14,)), dma((15,)),
+            dma((18,)), dma((19,)),
         ],
         compiler_params=pltpu.CompilerParams(vmem_limit_bytes=VMEM_LIMIT),
     )(act, a2a, grad, gright)

time: 111 us -> 112 us (level)
  no operation moved by 1% of the time
where the time goes in v7:
time: 112 us; the launch traced here: 111 us
  Pallas kernels  109 us (97%)
  other arithmetic  1.3 us (1%)
    pallas_call x1, Pallas kernels, fused(): pl.pallas_call(functools.partial(kernel, norm_scale), out_shape=(jax.Shap...  104 us
    pallas_call x1, Pallas kernels, place(): pl.pallas_call(functools.partial(place_kernel, wide), out_shape=(jax.Shap...  4.93 us

profile of v7, /device:TPU:0, one launch (start us, length us, event | category | flops | bytes accessed | tf_op | source)
XLA Modules:
  0.0 110.8 jit_solution(11967834725969342967)
XLA Ops:
  0.6 0.7 compare_select_fusion
  1.3 0.6 select_reduce_fusion.refs_0_
  1.9 103.8 %shard_map.101 = (bf16[8,2,32,3584]{3,2,1,0:T(8,128)(2,1)}, bf16[8,64,1024]{2,1,0:T(8,128)(2,1)}, f32[224,768]{1,0:T(8,128)}, f32[64,256]{1,0:T(8,128)}) custom-call(s32[64]{0:T(128)} %select_reduce_fusion.refs_0_, bf16[8,2,32,1024]{3,2,1,0:T(8,128)(2,1)} %bitcast.8, bf16[3584,512]{1,0:T(8,128)(2,1)} %refs_2_.1, bf16[3584,256]{1,0:T(8,128)(2,1)} %refs_3_.1, ...), custom_call_target="tpu_custom_call" | custom-call | tf_op jit(solution)/shard_map/pallas_call | solution.py:479
  105.7 4.9 %shard_map.102 = (bf16[512,3584]{1,0:T(8,128)(2,1)}, bf16[64,8192]{1,0:T(8,128)(2,1)}, f32[224,512]{1,0:T(8,128)}, f32[224,256]{1,0:T(8,128)}, f32[64,256]{1,0:T(8,128)}) custom-call(bf16[512,3584]{1,0:T(8,128)(2,1)} %bitcast.6, bf16[8,64,1024]{2,1,0:T(8,128)(2,1)} %get-tuple-element.15.a2a, f32[224,768]{1,0:T(8,128)} %get-tuple-element.16.grad, ...), custom_call_target="tpu_custom_call" | custom-call | tf_op jit(solution)/shard_map/pallas_call | solution.py:551
  (3 shorter events, 0.0 us)
